TPU v7x, 32 devices: a whole 2x2x4 slice. The times are simulated.
32 devices in a mesh: view: 2 (over core), gz: 8 (over z, y), gy: 2 (over x).
Axes of the slice: x: 2, y: 2, z: 4, core: 2. Of those that a mesh axis runs over, the one named last changes fastest.
Arguments:
- observed: float32 [2, 512, 32, 256], P('view', 'gz', 'gy'), may hold values from 0.5 to 4
- start: float32 [512, 32, 256], P('gz', 'gy'), may hold values from 0.5 to 2
- spread_z: float32 [2, 31], P('view'), may hold values from 0.05 to 1
- spread_y: float32 [2, 7], P('view'), may hold values from 0.1 to 1
- spread_x: float32 [2, 7], P('view'), may hold values from 0.1 to 1
Outputs:
- estimate: float32 [512, 32, 256], P('gz', 'gy')
All inputs are finite; a program needn't handle non-finite values.
Results may differ from a plain program's by a relative error of at most 0.0001.
Values sent between devices are 32-bit elements; how exact they have to be, the bound alone decides.
A program may use at most 64 MiB of HBM per device.

v0:
```python
import functools

import jax
import jax.numpy as jnp
from jax import lax
from jax.experimental import pallas as pl
from jax.experimental.pallas import tpu as pltpu
from jax.sharding import PartitionSpec as P

ITERS = 2
MESH = pl.DeviceIdType.MESH
F32 = jnp.float32
BF16 = jnp.bfloat16


def split(x):
    high = x.astype(BF16)
    return high, (x - high.astype(F32)).astype(BF16)


def kernel(dims, obs_hbm, start_hbm, sz_ref, sy_ref, sx_ref, out_hbm,
           raw_z, raw_y, raw_x, stage, obs_z, obs_t, mine, theirs, wf, wb, tx, zbuf, ybuf, qbuf,
           ebuf, cbuf, rybuf, rzbuf, lsem, osem, ssem, rsem, xssem, xrsem):
    NH, NY, NX, HZ, KZ, KY, KX, S, G = dims
    my, mz, mx = KY // 2, KZ // 2, KX // 2
    NE, NR = NH + 2 * HZ, NY + 2 * my
    v = lax.axis_index("view")
    gy = lax.axis_index("gy")
    s = 2 * lax.axis_index("gz") + v
    up_z, dn_z = s < S - 1, s > 0
    up_y, dn_y = gy < G - 1, gy > 0

    def zdev(t):
        t = lax.rem(t + S, S)
        return {"view": lax.rem(t, 2), "gz": t // 2}

    def ydev(t):
        return {"gy": lax.rem(t + G, G)}

    zto = (zdev(s + 1), zdev(s - 1))
    yto = (ydev(gy + 1), ydev(gy - 1))
    partner = {"view": 1 - v}
    zhas, yhas = (up_z, dn_z), (up_y, dn_y)
    zfrom, yfrom = (dn_z, up_z), (dn_y, up_y)

    load_start = pltpu.make_async_copy(start_hbm.at[pl.ds(v * NH, NH)], stage.at[0], lsem.at[0])
    load_start.start()
    load_obs = pltpu.make_async_copy(obs_hbm.at[0, pl.ds(v * NH, NH)], obs_z.at[v], lsem.at[1])
    load_obs.start()
    loads = [pltpu.make_async_copy(ref, raw, lsem.at[3 + row])
             for row, (ref, raw) in enumerate(((sz_ref, raw_z), (sy_ref, raw_y), (sx_ref, raw_x)))]
    for load in loads:
        load.start()

    barrier = pltpu.get_barrier_semaphore()
    for has, to in ((up_z, zto[0]), (dn_z, zto[1]), (up_y, yto[0]), (dn_y, yto[1])):
        @pl.when(has)
        def _(to=to):
            pl.semaphore_signal(barrier, inc=1, device_id=to, device_id_type=MESH)

    for it in range(ITERS):
        for d in range(2):
            @pl.when(jnp.logical_not(zfrom[d]))
            def _(it=it, d=d):
                z0 = (0, HZ + NH)[d]
                ebuf[it, :, z0:z0 + HZ, :] = jnp.zeros((NR, HZ, NX), F32)

            @pl.when(jnp.logical_not(yfrom[d]))
            def _(it=it, d=d):
                r0 = (0, my + NY)[d]
                ebuf[it, r0:r0 + my] = jnp.zeros((my, NE, NX), F32)

    load_start.wait()
    ebuf[0, my:my + NY, HZ:HZ + NH, :] = jnp.transpose(stage[0], (1, 0, 2))

    peers = sum(has.astype(jnp.int32) for has in (up_z, dn_z, up_y, dn_y))
    pl.semaphore_wait(barrier, peers)

    def copy(phase, m, src, dst, to):
        return pltpu.make_async_remote_copy(
            src_ref=src, dst_ref=dst, send_sem=ssem.at[phase, m], recv_sem=rsem.at[phase, m],
            device_id=to, device_id_type=MESH)

    CH = NY // 2
    ROWS = ((my, my), (NY, my), (2 * my, CH - 2 * my), (CH, 2 * my), (CH + 2 * my, NY - CH - 2 * my))
    NP = len(ROWS)
    ZED = ((HZ, NH), (0, HZ), (HZ + NH, HZ))
    ENDS = (0, 1)

    def when(cond, fn):
        @pl.when(cond)
        def _():
            fn()

    def both(a, b):
        return jnp.logical_and(a, b)

    zed_has = (None, dn_z, up_z)

    def gz(it, d, p):
        e = ebuf.at[it]
        src0, dst0 = ((NH, 0), (HZ, HZ + NH))[d]
        r0, n = ROWS[p]
        return copy(2 * it, NP * d + p, e.at[pl.ds(r0, n), pl.ds(src0, HZ)],
                    e.at[pl.ds(r0, n), pl.ds(dst0, HZ)], zto[d])

    def gyc(it, d, p):
        e = ebuf.at[it]
        src0, dst0 = ((NY, 0), (my, my + NY))[d]
        z0, n = ZED[p]
        return copy(2 * it, 2 * NP + 3 * d + p, e.at[pl.ds(src0, my), pl.ds(z0, n)],
                    e.at[pl.ds(dst0, my), pl.ds(z0, n)], yto[d])

    def sz(it, d, p):
        src0 = (HZ + NH, 0)[d]
        r0, n = ROWS[p]
        return copy(2 * it + 1, NP * d + p, cbuf.at[it, pl.ds(r0, n), pl.ds(src0, HZ)],
                    rzbuf.at[it, d, pl.ds(r0 - my, n)], zto[d])

    def sy(it, d, p):
        src0 = (my + NY, 0)[d]
        z0, n = ZED[p]
        return copy(2 * it + 1, 2 * NP + 3 * d + p, cbuf.at[it, pl.ds(src0, my), pl.ds(z0, n)],
                    rybuf.at[it, d, :, pl.ds(z0, n)], yto[d])

    def gather_piece(it, p):
        for d in range(2):
            when(zhas[d], gz(it, d, p).start)

    def gather_own(it):
        for d in range(2):
            when(yhas[d], gyc(it, d, 0).start)

    def gather_take(it, p):
        for d in range(2):
            when(zfrom[d], gz(it, d, p).wait_recv)
            if p in ENDS:
                dy = 1 - p
                when(both(zfrom[d], yhas[dy]), gyc(it, dy, 1 + d).start)

    def gather_edge(it, d):
        when(yfrom[d], gyc(it, d, 0).wait_recv)
        for q in range(2):
            when(both(zed_has[1 + q], yfrom[d]), gyc(it, d, 1 + q).wait_recv)

    def sent(it, z, y):
        for d in range(2):
            for p in range(NP):
                when(zhas[d], z(it, d, p).wait_send)
            when(yhas[d], y(it, d, 0).wait_send)
            for q in range(2):
                when(both(zed_has[1 + q], yhas[d]), y(it, d, 1 + q).wait_send)

    def scatter_edge(it, d):
        for q in range(2):
            when(both(zed_has[1 + q], yhas[d]), sy(it, d, 1 + q).start)
        when(yhas[d], sy(it, d, 0).start)

    def scatter_piece(it, p):
        for d in range(2):
            when(zhas[d], sz(it, d, p).start)

    def scatter_end(it, p):
        d, r0 = p, ROWS[p][0]
        for q in range(2):
            z0 = ZED[1 + q][0]

            def add(q=q, z0=z0):
                sy(it, d, 1 + q).wait_recv()
                cbuf[it, r0:r0 + my, z0:z0 + HZ, :] += rybuf[it, d, :, z0:z0 + HZ, :]
            when(both(zed_has[1 + q], yfrom[d]), add)
            when(zed_has[1 + q], sz(it, 1 - q, p).start)

    def scatter_take(it, p):
        r0, n = ROWS[p]
        if p in ENDS:
            def add_y():
                sy(it, p, 0).wait_recv()
                cbuf[it, r0:r0 + n, HZ:HZ + NH, :] += rybuf[it, p, :, HZ:HZ + NH, :]
            when(yfrom[p], add_y)
        for d in range(2):
            z0 = (HZ, NH)[d]

            def add_z(d=d, z0=z0):
                sz(it, d, p).wait_recv()
                cbuf[it, r0:r0 + n, z0:z0 + HZ, :] += rzbuf[it, d, r0 - my:r0 - my + n]
            when(zfrom[d], add_z)

    for p in range(NP):
        gather_piece(0, p)
    gather_own(0)
    mine[...] = jnp.zeros_like(mine)
    for row, (raw, taps) in enumerate(((raw_z, KZ), (raw_y, KY), (raw_x, KX))):
        loads[row].wait()
        mine[row:row + 1, 0:taps] = raw[...] / jnp.sum(raw[...], axis=1, keepdims=True)
    swap_prof = pltpu.make_async_remote_copy(
        src_ref=mine, dst_ref=theirs, send_sem=xssem.at[0], recv_sem=xrsem.at[0],
        device_id=partner, device_id_type=MESH)
    swap_prof.start()
    swap_obs = pltpu.make_async_remote_copy(
        src_ref=obs_hbm.at[0, pl.ds((1 - v) * NH, NH)], dst_ref=obs_z.at[v],
        send_sem=xssem.at[1], recv_sem=xrsem.at[1], device_id=partner, device_id_type=MESH)
    swap_obs.start()

    swap_prof.wait()
    own, other = mine[...], theirs[...]
    prof = (jnp.where(v == 0, own, other), jnp.where(v == 0, other, own))

    def tap(view, row, a):
        return prof[view][row:row + 1, a:a + 1]

    rows = lax.broadcasted_iota(jnp.int32, (NE, 3 * NE), 0)
    cols = lax.broadcasted_iota(jnp.int32, (NE, 3 * NE), 1)
    third = cols // NE
    cols = cols - third * NE

    def banded(diff, view, row, taps):
        w = jnp.zeros(diff.shape, F32)
        for a in range(taps):
            w = jnp.where(diff == a, tap(view, row, a), w)
        return w

    off = HZ - mz
    for ref, inner, outer in ((wf, rows, cols), (wb, cols, rows)):
        second = inner >= NH
        diff = outer - jnp.where(second, inner - NH, inner) - off
        w = jnp.where(second, banded(diff, 1, 0, KZ), banded(diff, 0, 0, KZ))
        high, low = split(w)
        ref[...] = jnp.where(third == 2, low.astype(F32), high.astype(F32)).astype(BF16)
    for view in range(2):
        for back in range(2):
            for r0 in range(0, NX, 64):
                r = lax.broadcasted_iota(jnp.int32, (64, NX), 0) + r0
                c = lax.broadcasted_iota(jnp.int32, (64, NX), 1)
                diff = (c - r if back else r - c) + mx
                high, low = split(banded(diff, view, 2, KX))
                tx[view, back, 0, r0:r0 + 64, :] = high
                tx[view, back, 1, r0:r0 + 64, :] = low
    wy = [[jnp.broadcast_to(tap(view, 1, b), (NH, NX)) for b in range(KY)] for view in range(2)]

    qbuf[0:2 * my] = jnp.zeros((2 * my, NE, NX), F32)
    qbuf[2 * my + NY:] = jnp.zeros((2 * my, NE, NX), F32)

    load_obs.wait()
    swap_obs.wait()
    for view in range(2):
        obs_t[view] = jnp.transpose(obs_z[view], (1, 0, 2))

    def xblur(view, back):
        high, low = ybuf[0], ybuf[1]
        both_ = jnp.concatenate([high, low], axis=0)
        n = high.shape[0]
        d = jnp.dot(both_, tx[view, back, 0], preferred_element_type=F32)
        d2 = jnp.dot(high, tx[view, back, 1], preferred_element_type=F32)
        return d[:n] + (d[n:] + d2)

    def stacked(x):
        high, low = split(x)
        return jnp.concatenate([high, low, high], axis=0)

    for it in range(ITERS):
        def zrow(y, carry, it=it):
            zbuf[y] = jnp.dot(wf[...], stacked(ebuf[it, y]), preferred_element_type=F32)
            return carry

        def zrows(r0, n):
            lax.fori_loop(r0, r0 + n, zrow, 0, unroll=True)

        def half(y0, it=it):
            for view in range(2):
                z0 = view * NH
                for y in range(CH):
                    acc = wy[view][0] * zbuf[y0 + y, z0:z0 + NH, :]
                    for b in range(1, KY):
                        acc = acc + wy[view][b] * zbuf[y0 + y + b, z0:z0 + NH, :]
                    high, low = split(acc)
                    ybuf[0, y * NH:(y + 1) * NH, :] = high
                    ybuf[1, y * NH:(y + 1) * NH, :] = low
                blurred = xblur(view, 0)
                quotient = obs_t[view, y0:y0 + CH].reshape(CH * NH, NX) / blurred
                high, low = split(quotient)
                ybuf[0] = high
                ybuf[1] = low
                qbuf[2 * my + y0:2 * my + y0 + CH, z0:z0 + NH, :] = xblur(view, 1).reshape(CH, NH, NX)

        def crow(r, carry, it=it):
            parts = []
            for view in range(2):
                z0 = view * NH
                acc = wy[view][0] * qbuf[r + 2 * my, z0:z0 + NH, :]
                for b in range(1, KY):
                    acc = acc + wy[view][b] * qbuf[r + 2 * my - b, z0:z0 + NH, :]
                parts.append(acc)
            cbuf[it, r] = jnp.dot(wb[...], stacked(jnp.concatenate(parts, axis=0)),
                                  preferred_element_type=F32)
            return carry
        def crows(r0, n):
            lax.fori_loop(r0, r0 + n, crow, 0, unroll=True)

        for p in ((0, 1, 2, 3) if it == 0 else (2, 0, 1, 3)):
            gather_take(it, p)
            zrows(*ROWS[p])
        gather_edge(it, 0)
        zrows(0, my)
        half(0)
        crows(0, my)
        scatter_edge(it, 1)
        crows(*ROWS[2])
        scatter_piece(it, 2)
        gather_take(it, 4)
        zrows(*ROWS[4])
        gather_edge(it, 1)
        zrows(my + NY, my)
        half(CH)
        crows(my + NY, my)
        scatter_edge(it, 0)
        for p in (3, 4):
            crows(*ROWS[p])
            scatter_piece(it, p)
        for p in ENDS:
            crows(*ROWS[p])
            scatter_end(it, p)

        def update(p, it=it):
            r0, n = ROWS[p]
            scatter_take(it, p)
            new = ebuf[it, r0:r0 + n, HZ:HZ + NH, :] * (0.5 * cbuf[it, r0:r0 + n, HZ:HZ + NH, :])
            if it + 1 < ITERS:
                ebuf[it + 1, r0:r0 + n, HZ:HZ + NH, :] = new
            else:
                zbuf[r0:r0 + n, 0:NH, :] = new

        if it + 1 < ITERS:
            update(2)
            gather_piece(it + 1, 2)
            update(3)
            update(4)
            update(0)
            gather_piece(it + 1, 0)
            update(1)
            gather_piece(it + 1, 1)
            gather_own(it + 1)
            gather_piece(it + 1, 3)
            gather_piece(it + 1, 4)
        else:
            outs = []
            for n, p in enumerate((2, 3, 4, 0, 1)):
                update(p)
                r0, rows_ = ROWS[p]
                src = zbuf.at[pl.ds(r0, rows_), pl.ds(0, NH)]
                dst = out_hbm.at[pl.ds(r0 - my, rows_), pl.ds(v * NH, NH)]
                outs.append(pltpu.make_async_copy(src, dst, osem.at[n]))
                outs.append(pltpu.make_async_remote_copy(
                    src_ref=src, dst_ref=dst, send_sem=xssem.at[2 + n], recv_sem=xrsem.at[2 + n],
                    device_id=partner, device_id_type=MESH))
                outs[-1].start()
                outs[-2].start()
            for out in outs:
                out.wait()
    for it in range(ITERS):
        sent(it, gz, gyc)
        sent(it, sz, sy)


def on_device(S, G, observed, start, spread_z, spread_y, spread_x):
    NZ, NY, NX = start.shape
    KZ, KY, KX = spread_z.shape[1], spread_y.shape[1], spread_x.shape[1]
    NH = NZ // 2
    my = KY // 2
    HZ = -(-(KZ // 2) // 8) * 8
    NE, NR = NH + 2 * HZ, NY + 2 * my
    dims = (NH, NY, NX, HZ, KZ, KY, KX, S, G)
    vm = pltpu.VMEM
    hbm = pl.BlockSpec(memory_space=pltpu.HBM)
    out = pl.pallas_call(
        functools.partial(kernel, dims),
        out_shape=jax.ShapeDtypeStruct((NY, NZ, NX), F32),
        in_specs=[hbm] * 5,
        out_specs=hbm,
        scratch_shapes=[
            vm((1, KZ), F32), vm((1, KY), F32), vm((1, KX), F32),
            vm((1, NH, NY, NX), F32), vm((2, NH, NY, NX), F32), vm((2, NY, NH, NX), F32),
            vm((8, 128), F32), vm((8, 128), F32),
            vm((NE, 3 * NE), BF16), vm((NE, 3 * NE), BF16), vm((2, 2, 2, NX, NX), BF16),
            vm((NR, NE, NX), F32), vm((2, NY // 2 * NH, NX), BF16), vm((NY + 4 * my, NE, NX), F32),
            vm((ITERS, NR, NE, NX), F32), vm((ITERS, NR, NE, NX), F32),
            vm((ITERS, 2, my, NE, NX), F32), vm((ITERS, 2, NY, HZ, NX), F32),
            pltpu.SemaphoreType.DMA((6,)), pltpu.SemaphoreType.DMA((5,)),
            pltpu.SemaphoreType.DMA((2 * ITERS, 16)), pltpu.SemaphoreType.DMA((2 * ITERS, 16)),
            pltpu.SemaphoreType.DMA((7,)), pltpu.SemaphoreType.DMA((7,)),
        ],
        compiler_params=pltpu.CompilerParams(
            collective_id=0, has_side_effects=True, vmem_limit_bytes=67043328),
    )(observed, start, spread_z, spread_y, spread_x)
    return jnp.transpose(out, (1, 0, 2))


def solution(mesh):
    S, G = 2 * mesh.shape["gz"], mesh.shape["gy"]
    return jax.shard_map(
        functools.partial(on_device, S, G),
        mesh=mesh,
        in_specs=(
            P("view", "gz", "gy", None),
            P("gz", "gy", None),
            P("view", None),
            P("view", None),
            P("view", None),
        ),
        out_specs=P("gz", "gy", None),
        check_vma=False,
    )
```

profile of v0, /device:TPU:13, one launch (start us, length us, event | category | flops | bytes accessed | tf_op | source)
XLA Modules:
  0.0 40.5 jit_solution(10493885689295133723)
XLA Ops:
  0.0 37.7 %shard_map.55 = f32[16,64,256]{2,1,0:T(8,128)} custom-call(f32[1,64,16,256]{3,2,1,0:T(8,128)} %obs_hbm.1, f32[64,16,256]{2,1,0:T(8,128)} %start_hbm.1, f32[1,31]{1,0:T(1,128)} %sz_ref.1, f32[1,7]{1,0:T(1,128)} %sy_ref.1, f32[1,7]{1,0:T(1,128)} %sx_ref.1), custom_call_target="tpu_custom_call" | custom-call | tf_op jit(solution)/shard_map/pallas_call | solution.py:375
  37.7 2.8 %copy.6 = f32[64,16,256]{2,1,0:T(8,128)} copy(f32[64,16,256]{2,0,1:T(8,128)} %bitcast.1) | data formatting | bytes 2097152 | tf_op jit(solution)/shard_map/transpose | solution.py:395
where the time goes:
time: 41.1 us; the launch traced here: 40.5 us
  Pallas kernels  37.7 us (92%)
  local copies, waits for them, and re-layouts  2.81 us (7%)
    pallas_call x1, Pallas kernels, on_device(): pl.pallas_call(functools.partial(kernel, dims), out_shape=jax.ShapeDtypeS...  37.7 us
    transpose x1, local copies, waits for them, and re-layouts, on_device(): return jnp.transpose(out, (1, 0, 2))  2.81 us

commit v1 on v0

v1 whole, which is shorter than its diff:
```python
import contextlib
import functools

import jax
import jax.numpy as jnp
from jax import lax
from jax.experimental import pallas as pl
from jax.experimental.pallas import tpu as pltpu
from jax.sharding import PartitionSpec as P

ITERS = 2
MESH = pl.DeviceIdType.MESH
F32 = jnp.float32
BF16 = jnp.bfloat16


def scope(name):
    return contextlib.nullcontext()


def split(x):
    high = x.astype(BF16)
    return high, (x - high.astype(F32)).astype(BF16)


def kernel(dims, obs_hbm, start_hbm, sz_ref, sy_ref, sx_ref, out_hbm,
           raw_z, raw_y, raw_x, stage, land, obs_z, obs_t, mine, theirs, wf, wb, tx, zbuf, ybuf, qbuf,
           ebuf, cbuf, rybuf, rzbuf, lsem, osem, gsem, hsem, ssem, rsem, xssem, xrsem):
    NH, NY, NX, HZ, KZ, KY, KX, S, G = dims
    my, mz, mx = KY // 2, KZ // 2, KX // 2
    NE, NR, NQ = NH + 2 * HZ, NY + 2 * my, NY + 4 * my
    CH = NY // 2
    v = lax.axis_index("view")
    gy = lax.axis_index("gy")
    s = 2 * lax.axis_index("gz") + v
    up_z, dn_z = s < S - 1, s > 0
    up_y, dn_y = gy < G - 1, gy > 0
    f = lax.rem(gy, 2)
    has = (jnp.logical_or(jnp.logical_and(f == 0, up_y), jnp.logical_and(f == 1, dn_y)),
           jnp.logical_or(jnp.logical_and(f == 0, dn_y), jnp.logical_and(f == 1, up_y)))

    def row(i0, n=1):
        return i0 + f * (NR - 2 * i0 - n)

    def qrow(j0, n=1):
        return j0 + f * (NQ - 2 * j0 - n)

    def zdev(t):
        t = lax.rem(t + S, S)
        return {"view": lax.rem(t, 2), "gz": t // 2}

    zto = (zdev(s + 1), zdev(s - 1))
    step = 1 - 2 * f
    yto = ({"gy": lax.rem(gy + step + G, G)}, {"gy": lax.rem(gy - step + G, G)})
    partner = {"view": 1 - v}
    zhas, zfrom = (up_z, dn_z), (dn_z, up_z)

    def when(cond, fn):
        @pl.when(cond)
        def _():
            fn()

    def both(a, b):
        return jnp.logical_and(a, b)

    barrier = pltpu.get_barrier_semaphore()
    for there, to in ((up_z, zto[0]), (dn_z, zto[1]), (has[0], yto[0]), (has[1], yto[1])):
        @pl.when(there)
        def _(to=to):
            pl.semaphore_signal(barrier, inc=1, device_id=to, device_id_type=MESH)

    load_start = pltpu.make_async_copy(start_hbm.at[pl.ds(v * NH, NH)], stage.at[0], lsem.at[0])
    load_start.start()
    load_obs = pltpu.make_async_copy(obs_hbm.at[0, pl.ds(v * NH, NH)], obs_z.at[v], lsem.at[1])
    load_obs.start()
    loads = [pltpu.make_async_copy(ref, raw, lsem.at[3 + k])
             for k, (ref, raw) in enumerate(((sz_ref, raw_z), (sy_ref, raw_y), (sx_ref, raw_x)))]
    for load in loads:
        load.start()

    blocks = (CH * (1 - f), CH * f)

    def first(d, k):
        b0 = pl.multiple_of(blocks[k], CH)
        src0 = v * NH + (NH - mz, 0)[d]
        dst0 = (HZ - mz, 0)[d]
        return pltpu.make_async_remote_copy(
            src_ref=start_hbm.at[pl.ds(src0, mz), pl.ds(b0, CH)],
            dst_ref=land.at[d, pl.ds(dst0, mz), pl.ds(b0, CH)],
            send_sem=gsem.at[d, k], recv_sem=hsem.at[d, k], device_id=zto[d], device_id_type=MESH)

    peers = sum(there.astype(jnp.int32) for there in (up_z, dn_z, has[0], has[1]))
    with scope("Wbar"):
        pl.semaphore_wait(barrier, peers)
    for k in range(2):
        for d in range(2):
            when(zhas[d], first(d, k).start)

    land[0, 0:HZ - mz] = jnp.zeros((HZ - mz, NY, NX), F32)
    land[1, mz:HZ] = jnp.zeros((HZ - mz, NY, NX), F32)
    for d in range(2):
        def blank(d=d):
            for it in range(ITERS):
                z0 = (0, HZ + NH)[d]
                ebuf[it, :, z0:z0 + HZ, :] = jnp.zeros((NR, HZ, NX), F32)
        when(jnp.logical_not(zfrom[d]), blank)

        def blank_rows(d=d):
            zbuf[pl.ds(row((my + NY, 0)[d], my), my)] = jnp.zeros((my, NE, NX), F32)
        when(jnp.logical_not(has[d]), blank_rows)

    def copy(phase, m, src, dst, to):
        return pltpu.make_async_remote_copy(
            src_ref=src, dst_ref=dst, send_sem=ssem.at[phase, m], recv_sem=rsem.at[phase, m],
            device_id=to, device_id_type=MESH)

    ROWS = ((NY, my), (my, my), (2 * my, CH - 2 * my), (CH, 2 * my), (CH + 2 * my, NY - CH - 2 * my))
    NP = len(ROWS)
    ZED = ((HZ, NH), (0, HZ), (HZ + NH, HZ))
    zed_has = (None, dn_z, up_z)
    EDGE, HALO = (NY, my), (my + NY, 0)
    THERE = (f * (my + NY), (1 - f) * (my + NY))

    def gz(it, d, p):
        e = ebuf.at[it]
        src0, dst0 = ((NH, 0), (HZ, HZ + NH))[d]
        n = ROWS[p][1]
        r0 = row(*ROWS[p])
        return copy(2 * it, NP * d + p, e.at[pl.ds(r0, n), pl.ds(src0, HZ)],
                    e.at[pl.ds(r0, n), pl.ds(dst0, HZ)], zto[d])

    def gyc(it, d, p):
        e = ebuf.at[it]
        z0, n = ZED[p]
        return copy(2 * it, 2 * NP + 3 * d + p, e.at[pl.ds(row(EDGE[d], my), my), pl.ds(z0, n)],
                    e.at[pl.ds(THERE[d], my), pl.ds(z0, n)], yto[d])

    def sz(it, d, p):
        src0 = (HZ + NH, 0)[d]
        n = ROWS[p][1]
        r0 = row(*ROWS[p])
        return copy(2 * it + 1, NP * d + p, cbuf.at[it, pl.ds(r0, n), pl.ds(src0, HZ)],
                    rzbuf.at[it, d, pl.ds(r0 - my, n)], zto[d])

    def sy(it, d, p):
        z0, n = ZED[p]
        return copy(2 * it + 1, 2 * NP + 3 * d + p, cbuf.at[it, pl.ds(row(HALO[d], my), my), pl.ds(z0, n)],
                    rybuf.at[it, d, :, pl.ds(z0, n)], yto[d])

    def gather_piece(it, p):
        for d in range(2):
            when(zhas[d], gz(it, d, p).start)

    def gather_own(it):
        for d in range(2):
            when(has[d], gyc(it, d, 0).start)

    def relay(it, p, d):
        if p < 2:
            when(both(zfrom[d], has[p]), gyc(it, p, 1 + d).start)

    def gather_take(it, p):
        for d in range(2):
            when(zfrom[d], gz(it, d, p).wait_recv)
            relay(it, p, d)

    def first_take(k):
        b0 = pl.multiple_of(blocks[k], CH)
        for d in range(2):
            z0 = (0, HZ + NH)[d]

            def take(d=d, z0=z0):
                first(d, k).wait_recv()
                ebuf[0, pl.ds(my + b0, CH), z0:z0 + HZ, :] = jnp.transpose(land[d, :, pl.ds(b0, CH), :], (1, 0, 2))
            when(zfrom[d], take)
            relay(0, k, d)

    def gather_edge(it, d):
        when(has[d], gyc(it, d, 0).wait_recv)
        for q in range(2):
            when(both(zed_has[1 + q], has[d]), gyc(it, d, 1 + q).wait_recv)

            def blank(q=q):
                z0 = ZED[1 + q][0]
                ebuf[it, pl.ds(row(HALO[d], my), my), z0:z0 + HZ, :] = jnp.zeros((my, HZ, NX), F32)

    def sent(it):
        for d in range(2):
            for p in range(NP):
                if it > 0:
                    when(zhas[d], gz(it, d, p).wait_send)
                when(zhas[d], sz(it, d, p).wait_send)
            for y in (gyc, sy):
                when(has[d], y(it, d, 0).wait_send)
                for q in range(2):
                    when(both(zed_has[1 + q], has[d]), y(it, d, 1 + q).wait_send)

    def scatter_edge(it, d):
        for q in range(2):
            when(both(zed_has[1 + q], has[d]), sy(it, d, 1 + q).start)
        when(has[d], sy(it, d, 0).start)

    def scatter_piece(it, p):
        for d in range(2):
            when(zhas[d], sz(it, d, p).start)

    def scatter_end(it, p):
        r0 = row(*ROWS[p])
        for q in range(2):
            z0 = ZED[1 + q][0]

            def add(q=q, z0=z0):
                sy(it, p, 1 + q).wait_recv()
                cbuf[it, pl.ds(r0, my), z0:z0 + HZ, :] += rybuf[it, p, :, z0:z0 + HZ, :]
            when(both(zed_has[1 + q], has[p]), add)
            when(zed_has[1 + q], sz(it, 1 - q, p).start)

    def scatter_take(it, p):
        n = ROWS[p][1]
        r0 = row(*ROWS[p])
        if p < 2:
            def add_y():
                sy(it, p, 0).wait_recv()
                cbuf[it, pl.ds(r0, n), HZ:HZ + NH, :] += rybuf[it, p, :, HZ:HZ + NH, :]
            when(has[p], add_y)
        for d in range(2):
            z0 = (HZ, NH)[d]

            def add_z(d=d, z0=z0):
                sz(it, d, p).wait_recv()
                cbuf[it, pl.ds(r0, n), z0:z0 + HZ, :] += rzbuf[it, d, pl.ds(r0 - my, n)]
            when(zfrom[d], add_z)

    with scope("Wload"):
        load_start.wait()
    ebuf[0, my:my + NY, HZ:HZ + NH, :] = jnp.transpose(stage[0], (1, 0, 2))
    gather_own(0)
    mine[...] = jnp.zeros_like(mine)
    for k, (raw, taps) in enumerate(((raw_z, KZ), (raw_y, KY), (raw_x, KX))):
        loads[k].wait()
        mine[k:k + 1, 0:taps] = raw[...] / jnp.sum(raw[...], axis=1, keepdims=True)
    swap_prof = pltpu.make_async_remote_copy(
        src_ref=mine, dst_ref=theirs, send_sem=xssem.at[0], recv_sem=xrsem.at[0],
        device_id=partner, device_id_type=MESH)
    swap_prof.start()
    swap_obs = pltpu.make_async_remote_copy(
        src_ref=obs_hbm.at[0, pl.ds((1 - v) * NH, NH)], dst_ref=obs_z.at[v],
        send_sem=xssem.at[1], recv_sem=xrsem.at[1], device_id=partner, device_id_type=MESH)
    swap_obs.start()

    with scope("Wprof"):
        swap_prof.wait()
    own, other = mine[...], theirs[...]
    prof = (jnp.where(v == 0, own, other), jnp.where(v == 0, other, own))

    def tap(view, k, a):
        return prof[view][k:k + 1, a:a + 1]

    rows = lax.broadcasted_iota(jnp.int32, (NE, 3 * NE), 0)
    cols = lax.broadcasted_iota(jnp.int32, (NE, 3 * NE), 1)
    third = cols // NE
    cols = cols - third * NE

    def banded(diff, view, k, taps):
        w = jnp.zeros(diff.shape, F32)
        for a in range(taps):
            w = jnp.where(diff == a, tap(view, k, a), w)
        return w

    off = HZ - mz
    for ref, inner, outer in ((wf, rows, cols), (wb, cols, rows)):
        second = inner >= NH
        diff = outer - jnp.where(second, inner - NH, inner) - off
        w = jnp.where(second, banded(diff, 1, 0, KZ), banded(diff, 0, 0, KZ))
        high, low = split(w)
        ref[...] = jnp.where(third == 2, low.astype(F32), high.astype(F32)).astype(BF16)
    for view in range(2):
        for back in range(2):
            for r0 in range(0, NX, 64):
                r = lax.broadcasted_iota(jnp.int32, (64, NX), 0) + r0
                c = lax.broadcasted_iota(jnp.int32, (64, NX), 1)
                diff = (c - r if back else r - c) + mx
                high, low = split(banded(diff, view, 2, KX))
                tx[view, back, 0, r0:r0 + 64, :] = high
                tx[view, back, 1, r0:r0 + 64, :] = low
    wy = [[jnp.broadcast_to(tap(view, 1, b), (NH, NX)) for b in range(KY)] for view in range(2)]

    qbuf[0:2 * my] = jnp.zeros((2 * my, NE, NX), F32)
    qbuf[2 * my + NY:] = jnp.zeros((2 * my, NE, NX), F32)

    with scope("Wobs"):
        load_obs.wait()
        swap_obs.wait()
    for view in range(2):
        obs_t[view] = jnp.transpose(obs_z[view], (1, 0, 2))

    def xblur(high, low, view, back):
        both_ = jnp.concatenate([high, low], axis=0)
        n = high.shape[0]
        d = jnp.dot(both_, tx[view, back, 0], preferred_element_type=F32)
        d2 = jnp.dot(high, tx[view, back, 1], preferred_element_type=F32)
        return d[:n] + (d[n:] + d2)

    def stacked(x):
        high, low = split(x)
        return jnp.concatenate([high, low, high], axis=0)

    for it in range(ITERS):
        def zrows(i0, n, it=it):
            with scope(f"z{it}_{i0}"):
                r0 = row(i0, n)
                for y in range(n):
                    zbuf[r0 + y] = jnp.dot(wf[...], stacked(ebuf[it, r0 + y]), preferred_element_type=F32)

        def qrows(o0, n, it=it):
            with scope(f"q{it}_{o0}"):
                y0 = row(o0 + my, n) - my
                for view in range(2):
                    z0 = view * NH
                    for y in range(n):
                        acc = wy[view][0] * zbuf[y0 + y, z0:z0 + NH, :]
                        for b in range(1, KY):
                            acc = acc + wy[view][b] * zbuf[y0 + y + b, z0:z0 + NH, :]
                        high, low = split(acc)
                        ybuf[view, 0, y * NH:(y + 1) * NH, :] = high
                        ybuf[view, 1, y * NH:(y + 1) * NH, :] = low
                for view in range(2):
                    z0 = view * NH
                    m = n * NH
                    blurred = xblur(ybuf[view, 0, 0:m], ybuf[view, 1, 0:m], view, 0)
                    quotient = obs_t[view, pl.ds(y0, n)].reshape(m, NX) / blurred
                    high, low = split(quotient)
                    ybuf[view, 2, 0:m] = high
                    ybuf[view, 3, 0:m] = low
                    qbuf[pl.ds(2 * my + y0, n), z0:z0 + NH, :] = xblur(
                        ybuf[view, 2, 0:m], ybuf[view, 3, 0:m], view, 1).reshape(n, NH, NX)

        def crows(i0, n, it=it):
            with scope(f"c{it}_{i0}"):
                r0 = row(i0, n)
                for y in range(n):
                    r = r0 + y
                    parts = []
                    for view in range(2):
                        z0 = view * NH
                        acc = wy[view][0] * qbuf[r + 2 * my, z0:z0 + NH, :]
                        for b in range(1, KY):
                            acc = acc + wy[view][b] * qbuf[r + 2 * my - b, z0:z0 + NH, :]
                        parts.append(acc)
                    cbuf[it, r] = jnp.dot(wb[...], stacked(jnp.concatenate(parts, axis=0)),
                                          preferred_element_type=F32)

        if it == 0:
            with scope("Wg0_in"):
                first_take(0)
            zrows(my + CH, CH)
            with scope("Wg0_out"):
                first_take(1)
            zrows(my, CH)
        else:
            for p in (2, 1, 3):
                with scope(f"Wg{it}_{p}"):
                    gather_take(it, p)
                zrows(*ROWS[p])

        def low_edge(it=it):
            gather_edge(it, 1)
            zrows(0, my)
        when(has[1], low_edge)
        qrows(0, CH)

        def low_scatter(it=it):
            crows(0, my)
            scatter_edge(it, 1)
        when(has[1], low_scatter)
        crows(*ROWS[1])
        when(jnp.logical_not(has[1]), functools.partial(scatter_piece, it, 1))
        crows(*ROWS[2])
        scatter_piece(it, 2)
        if it > 0:
            for p in (0, 4):
                with scope(f"Wg{it}_{p}"):
                    gather_take(it, p)
                zrows(*ROWS[p])

        def high_edge(it=it):
            with scope(f"Wge{it}"):
                gather_edge(it, 0)
            zrows(my + NY, my)
        when(has[0], high_edge)
        qrows(CH, CH)

        def high_scatter(it=it):
            crows(my + NY, my)
            scatter_edge(it, 0)
        when(has[0], high_scatter)
        for p in (3, 4):
            crows(*ROWS[p])
            scatter_piece(it, p)
        crows(*ROWS[0])
        with scope(f"Wse{it}"):
            when(has[1], functools.partial(scatter_end, it, 1))
            scatter_end(it, 0)

        def update(p, it=it):
            n = ROWS[p][1]
            r0 = row(*ROWS[p])
            with scope(f"Wst{it}_{p}"):
                scatter_take(it, p)
            new = ebuf[it, pl.ds(r0, n), HZ:HZ + NH, :] * (0.5 * cbuf[it, pl.ds(r0, n), HZ:HZ + NH, :])
            if it + 1 < ITERS:
                ebuf[it + 1, pl.ds(r0, n), HZ:HZ + NH, :] = new
            else:
                zbuf[pl.ds(r0, n), 0:NH, :] = new

        if it + 1 < ITERS:
            for p in (1, 2, 3):
                update(p)
                gather_piece(it + 1, p)
            update(0)
            gather_piece(it + 1, 0)
            gather_own(it + 1)
            update(4)
            gather_piece(it + 1, 4)
        else:
            outs = []
            for n, p in enumerate((1, 2, 3, 4, 0)):
                update(p)
                r0 = row(*ROWS[p])
                rows_ = ROWS[p][1]
                src = zbuf.at[pl.ds(r0, rows_), pl.ds(0, NH)]
                dst = out_hbm.at[pl.ds(r0 - my, rows_), pl.ds(v * NH, NH)]
                outs.append(pltpu.make_async_copy(src, dst, osem.at[n]))
                outs.append(pltpu.make_async_remote_copy(
                    src_ref=src, dst_ref=dst, send_sem=xssem.at[2 + n], recv_sem=xrsem.at[2 + n],
                    device_id=partner, device_id_type=MESH))
                outs[-1].start()
                outs[-2].start()
            with scope("Wout"):
                for out in outs:
                    out.wait()
    for it in range(ITERS):
        sent(it)
    for k in range(2):
        for d in range(2):
            when(zhas[d], first(d, k).wait_send)


def on_device(S, G, observed, start, spread_z, spread_y, spread_x):
    NZ, NY, NX = start.shape
    KZ, KY, KX = spread_z.shape[1], spread_y.shape[1], spread_x.shape[1]
    NH = NZ // 2
    my = KY // 2
    HZ = -(-(KZ // 2) // 8) * 8
    NE, NR = NH + 2 * HZ, NY + 2 * my
    dims = (NH, NY, NX, HZ, KZ, KY, KX, S, G)
    vm = pltpu.VMEM
    hbm = pl.BlockSpec(memory_space=pltpu.HBM)
    out = pl.pallas_call(
        functools.partial(kernel, dims),
        out_shape=jax.ShapeDtypeStruct((NY, NZ, NX), F32),
        in_specs=[hbm] * 5,
        out_specs=hbm,
        scratch_shapes=[
            vm((1, KZ), F32), vm((1, KY), F32), vm((1, KX), F32),
            vm((1, NH, NY, NX), F32), vm((2, HZ, NY, NX), F32),
            vm((2, NH, NY, NX), F32), vm((2, NY, NH, NX), F32),
            vm((8, 128), F32), vm((8, 128), F32),
            vm((NE, 3 * NE), BF16), vm((NE, 3 * NE), BF16), vm((2, 2, 2, NX, NX), BF16),
            vm((NR, NE, NX), F32), vm((2, 4, NY // 2 * NH, NX), BF16), vm((NY + 4 * my, NE, NX), F32),
            vm((ITERS, NR, NE, NX), F32), vm((ITERS, NR, NE, NX), F32),
            vm((ITERS, 2, my, NE, NX), F32), vm((ITERS, 2, NY, HZ, NX), F32),
            pltpu.SemaphoreType.DMA((6,)), pltpu.SemaphoreType.DMA((5,)),
            pltpu.SemaphoreType.DMA((2, 2)), pltpu.SemaphoreType.DMA((2, 2)),
            pltpu.SemaphoreType.DMA((2 * ITERS, 16)), pltpu.SemaphoreType.DMA((2 * ITERS, 16)),
            pltpu.SemaphoreType.DMA((7,)), pltpu.SemaphoreType.DMA((7,)),
        ],
        compiler_params=pltpu.CompilerParams(
            collective_id=0, has_side_effects=True, vmem_limit_bytes=67043328),
    )(observed, start, spread_z, spread_y, spread_x)
    return jnp.transpose(out, (1, 0, 2))


def solution(mesh):
    S, G = 2 * mesh.shape["gz"], mesh.shape["gy"]
    return jax.shard_map(
        functools.partial(on_device, S, G),
        mesh=mesh,
        in_specs=(
            P("view", "gz", "gy", None),
            P("gz", "gy", None),
            P("view", None),
            P("view", None),
            P("view", None),
        ),
        out_specs=P("gz", "gy", None),
        check_vma=False,
    )
```

time: 41.1 us -> 42.7 us (1.039)
  the two profiles are of different devices: /device:TPU:13 before, /device:TPU:19 now
where the time goes in v1:
time: 42.7 us; the launch traced here: 42.5 us
  Pallas kernels  39.7 us (93%)
  local copies, waits for them, and re-layouts  2.81 us (7%)
    pallas_call x1, Pallas kernels, on_device(): pl.pallas_call(functools.partial(kernel, dims), out_shape=jax.ShapeDtypeS...  39.7 us
    transpose x1, local copies, waits for them, and re-layouts, on_device(): return jnp.transpose(out, (1, 0, 2))  2.81 us

profile of v1, /device:TPU:19, one launch (start us, length us, event | category | flops | bytes accessed | tf_op | source)
XLA Modules:
  0.0 42.5 jit_solution(5623293560972421747)
XLA Ops:
  0.0 39.7 %shard_map.55 = f32[16,64,256]{2,1,0:T(8,128)} custom-call(f32[1,64,16,256]{3,2,1,0:T(8,128)} %obs_hbm.1, f32[64,16,256]{2,1,0:T(8,128)} %start_hbm.1, f32[1,31]{1,0:T(1,128)} %sz_ref.1, f32[1,7]{1,0:T(1,128)} %sy_ref.1, f32[1,7]{1,0:T(1,128)} %sx_ref.1), custom_call_target="tpu_custom_call" | custom-call | tf_op jit(solution)/shard_map/pallas_call | solution.py:459
  39.7 2.8 %copy.6 = f32[64,16,256]{2,1,0:T(8,128)} copy(f32[64,16,256]{2,0,1:T(8,128)} %bitcast.1) | data formatting | bytes 2097152 | tf_op jit(solution)/shard_map/transpose | solution.py:481

commit v2 on v1

--- a/solution.py
+++ b/solution.py
@@ -25,7 +25,7 @@
 
 def kernel(dims, obs_hbm, start_hbm, sz_ref, sy_ref, sx_ref, out_hbm,
            raw_z, raw_y, raw_x, stage, land, obs_z, obs_t, mine, theirs, wf, wb, tx, zbuf, ybuf, qbuf,
-           ebuf, cbuf, rybuf, rzbuf, lsem, osem, gsem, hsem, ssem, rsem, xssem, xrsem):
+           ebuf, cbuf, rybuf, rzbuf, sbuf, lsem, osem, gsem, hsem, ssem, rsem, xssem, xrsem):
     NH, NY, NX, HZ, KZ, KY, KX, S, G = dims
     my, mz, mx = KY // 2, KZ // 2, KX // 2
     NE, NR, NQ = NH + 2 * HZ, NY + 2 * my, NY + 4 * my
@@ -53,6 +53,8 @@
     step = 1 - 2 * f
     yto = ({"gy": lax.rem(gy + step + G, G)}, {"gy": lax.rem(gy - step + G, G)})
     partner = {"view": 1 - v}
+    zout = dict(zdev(s - 1 + 2 * v))
+    diag = tuple({**zout, **yto[d]} for d in range(2))
     zhas, zfrom = (up_z, dn_z), (dn_z, up_z)
 
     def when(cond, fn):
@@ -64,7 +66,8 @@
         return jnp.logical_and(a, b)
 
     barrier = pltpu.get_barrier_semaphore()
-    for there, to in ((up_z, zto[0]), (dn_z, zto[1]), (has[0], yto[0]), (has[1], yto[1])):
+    greet = ((up_z, zto[0]), (dn_z, zto[1]), (has[0], yto[0]), (has[1], yto[1]))
+    for there, to in greet:
         @pl.when(there)
         def _(to=to):
             pl.semaphore_signal(barrier, inc=1, device_id=to, device_id_type=MESH)
@@ -89,7 +92,7 @@
             dst_ref=land.at[d, pl.ds(dst0, mz), pl.ds(b0, CH)],
             send_sem=gsem.at[d, k], recv_sem=hsem.at[d, k], device_id=zto[d], device_id_type=MESH)
 
-    peers = sum(there.astype(jnp.int32) for there in (up_z, dn_z, has[0], has[1]))
+    peers = sum(there.astype(jnp.int32) for there, _ in greet)
     with scope("Wbar"):
         pl.semaphore_wait(barrier, peers)
     for k in range(2):
@@ -114,7 +117,8 @@
             src_ref=src, dst_ref=dst, send_sem=ssem.at[phase, m], recv_sem=rsem.at[phase, m],
             device_id=to, device_id_type=MESH)
 
-    ROWS = ((NY, my), (my, my), (2 * my, CH - 2 * my), (CH, 2 * my), (CH + 2 * my, NY - CH - 2 * my))
+    ROWS = ((NY, my), (my, my), (2 * my, NY - 4 * my), (NY - 2 * my, my), (NY - my, my))
+    OUT, MID = NY - 3 * my, 2 * my
     NP = len(ROWS)
     ZED = ((HZ, NH), (0, HZ), (HZ + NH, HZ))
     zed_has = (None, dn_z, up_z)
@@ -135,6 +139,22 @@
         return copy(2 * it, 2 * NP + 3 * d + p, e.at[pl.ds(row(EDGE[d], my), my), pl.ds(z0, n)],
                     e.at[pl.ds(THERE[d], my), pl.ds(z0, n)], yto[d])
 
+    def fwd(it, d, q):
+        rows_ = pl.ds(row(HALO[d], my), my)
+        e = ebuf.at[it]
+        return copy(2 * it, 2 * NP + 6 + 2 * d + q, e.at[rows_, pl.ds((NH, HZ)[q], HZ)],
+                    e.at[rows_, pl.ds((0, HZ + NH)[q], HZ)], partner)
+
+    def sfwd(it, d, q):
+        rows_ = pl.ds(row(HALO[d], my), my)
+        return copy(2 * it + 1, 2 * NP + 6 + 2 * d + q, cbuf.at[it, rows_, pl.ds((HZ + NH, 0)[q], HZ)],
+                    sbuf.at[it, d], partner)
+
+    def diagonal(it, d, q):
+        z0, n = ZED[1 + q]
+        return copy(2 * it + 1, 2 * NP + 3 * d + 1 + q, cbuf.at[it, pl.ds(row(HALO[d], my), my), pl.ds(z0, n)],
+                    rybuf.at[it, d, :, pl.ds(0, HZ)], diag[d])
+
     def sz(it, d, p):
         src0 = (HZ + NH, 0)[d]
         n = ROWS[p][1]
@@ -157,7 +177,7 @@
 
     def relay(it, p, d):
         if p < 2:
-            when(both(zfrom[d], has[p]), gyc(it, p, 1 + d).start)
+            when(both(both(zfrom[d], has[p]), v == d), gyc(it, p, 1 + d).start)
 
     def gather_take(it, p):
         for d in range(2):
@@ -175,14 +195,17 @@
             when(zfrom[d], take)
             relay(0, k, d)
 
+    def edge_own(it, d):
+        def go():
+            gyc(it, d, 0).wait_recv()
+            for q in range(2):
+                when(v == q, fwd(it, d, q).start)
+        when(has[d], go)
+
     def gather_edge(it, d):
-        when(has[d], gyc(it, d, 0).wait_recv)
         for q in range(2):
-            when(both(zed_has[1 + q], has[d]), gyc(it, d, 1 + q).wait_recv)
-
-            def blank(q=q):
-                z0 = ZED[1 + q][0]
-                ebuf[it, pl.ds(row(HALO[d], my), my), z0:z0 + HZ, :] = jnp.zeros((my, HZ, NX), F32)
+            when(both(both(zed_has[1 + q], has[d]), v == q), gyc(it, d, 1 + q).wait_recv)
+            when(both(has[d], v == 1 - q), fwd(it, d, q).wait_recv)
 
     def sent(it):
         for d in range(2):
@@ -193,11 +216,26 @@
             for y in (gyc, sy):
                 when(has[d], y(it, d, 0).wait_send)
                 for q in range(2):
-                    when(both(zed_has[1 + q], has[d]), y(it, d, 1 + q).wait_send)
+                    corner = diagonal(it, d, q) if y is sy and it + 1 == ITERS else y(it, d, 1 + q)
+                    when(both(both(zed_has[1 + q], has[d]), v == q), corner.wait_send)
+            for y in (fwd, sfwd):
+                for q in range(2):
+                    when(both(has[d], v == q), y(it, d, q).wait_send)
 
     def scatter_edge(it, d):
         for q in range(2):
-            when(both(zed_has[1 + q], has[d]), sy(it, d, 1 + q).start)
+            corner = diagonal(it, d, q) if it + 1 == ITERS else sy(it, d, 1 + q)
+            when(both(both(zed_has[1 + q], has[d]), v == q), corner.start)
+            when(both(has[d], v == q), sfwd(it, d, q).start)
+
+    def scatter_own(it, d):
+        r0 = row(HALO[d], my)
+        for q in range(2):
+            def add(q=q):
+                z0 = (HZ, NH)[q]
+                sfwd(it, d, q).wait_recv()
+                cbuf[it, pl.ds(r0, my), z0:z0 + HZ, :] += sbuf[it, d]
+            when(both(has[d], v == 1 - q), add)
         when(has[d], sy(it, d, 0).start)
 
     def scatter_piece(it, p):
@@ -212,8 +250,12 @@
             def add(q=q, z0=z0):
                 sy(it, p, 1 + q).wait_recv()
                 cbuf[it, pl.ds(r0, my), z0:z0 + HZ, :] += rybuf[it, p, :, z0:z0 + HZ, :]
-            when(both(zed_has[1 + q], has[p]), add)
-            when(zed_has[1 + q], sz(it, 1 - q, p).start)
+            when(both(both(zed_has[1 + q], has[p]), v == q), add)
+            when(both(zed_has[1 + q], v == q), sz(it, 1 - q, p).start)
+
+    def scatter_near(it, p):
+        for q in range(2):
+            when(v == 1 - q, sz(it, 1 - q, p).start)
 
     def scatter_take(it, p):
         n = ROWS[p][1]
@@ -223,6 +265,13 @@
                 sy(it, p, 0).wait_recv()
                 cbuf[it, pl.ds(r0, n), HZ:HZ + NH, :] += rybuf[it, p, :, HZ:HZ + NH, :]
             when(has[p], add_y)
+            if it + 1 == ITERS:
+                for q in range(2):
+                    def add_diagonal(q=q):
+                        z0 = (NH, HZ)[q]
+                        diagonal(it, p, q).wait_recv()
+                        cbuf[it, pl.ds(r0, n), z0:z0 + HZ, :] += rybuf[it, p, :, 0:HZ, :]
+                    when(both(both(zed_has[2 - q], has[p]), v == 1 - q), add_diagonal)
         for d in range(2):
             z0 = (HZ, NH)[d]
 
@@ -354,53 +403,84 @@
             with scope("Wg0_in"):
                 first_take(0)
             zrows(my + CH, CH)
+            with scope("Wge0own"):
+                edge_own(it, 0)
             with scope("Wg0_out"):
                 first_take(1)
             zrows(my, CH)
         else:
-            for p in (2, 1, 3):
+            for p in (1, 2, 3):
                 with scope(f"Wg{it}_{p}"):
                     gather_take(it, p)
                 zrows(*ROWS[p])
 
         def low_edge(it=it):
+            edge_own(it, 1)
             gather_edge(it, 1)
             zrows(0, my)
         when(has[1], low_edge)
-        qrows(0, CH)
-
         def low_scatter(it=it):
             crows(0, my)
             scatter_edge(it, 1)
-        when(has[1], low_scatter)
-        crows(*ROWS[1])
-        when(jnp.logical_not(has[1]), functools.partial(scatter_piece, it, 1))
-        crows(*ROWS[2])
-        scatter_piece(it, 2)
-        if it > 0:
-            for p in (0, 4):
-                with scope(f"Wg{it}_{p}"):
-                    gather_take(it, p)
-                zrows(*ROWS[p])
 
         def high_edge(it=it):
             with scope(f"Wge{it}"):
                 gather_edge(it, 0)
             zrows(my + NY, my)
-        when(has[0], high_edge)
-        qrows(CH, CH)
 
         def high_scatter(it=it):
             crows(my + NY, my)
             scatter_edge(it, 0)
-        when(has[0], high_scatter)
-        for p in (3, 4):
-            crows(*ROWS[p])
-            scatter_piece(it, p)
-        crows(*ROWS[0])
-        with scope(f"Wse{it}"):
-            when(has[1], functools.partial(scatter_end, it, 1))
-            scatter_end(it, 0)
+
+        qrows(0, OUT)
+        when(has[1], low_scatter)
+        crows(*ROWS[1])
+        when(jnp.logical_not(has[1]), functools.partial(scatter_piece, it, 1))
+        if it == 0:
+            qrows(OUT, MID)
+            for p in (2, 3):
+                crows(*ROWS[p])
+                scatter_piece(it, p)
+            when(has[0], high_edge)
+            qrows(OUT + MID, my)
+            when(has[0], high_scatter)
+            crows(*ROWS[4])
+            scatter_piece(it, 4)
+            crows(*ROWS[0])
+            scatter_near(it, 0)
+            with scope(f"Wse{it}"):
+                scatter_end(it, 0)
+            scatter_own(it, 0)
+        else:
+            with scope(f"Wg{it}_0"):
+                gather_take(it, 0)
+            zrows(*ROWS[0])
+            with scope(f"Wge{it}own"):
+                edge_own(it, 0)
+            with scope(f"Wg{it}_4"):
+                gather_take(it, 4)
+            zrows(*ROWS[4])
+            qrows(OUT, MID)
+            for p in (2, 3):
+                crows(*ROWS[p])
+                scatter_piece(it, p)
+            when(has[0], high_edge)
+            qrows(OUT + MID, my)
+            when(has[0], high_scatter)
+            for p in (0, 4):
+                crows(*ROWS[p])
+                scatter_piece(it, p)
+            with scope(f"Wso{it}"):
+                scatter_own(it, 0)
+
+        def low_end(it=it):
+            scatter_own(it, 1)
+            if it + 1 < ITERS:
+                scatter_near(it, 1)
+                scatter_end(it, 1)
+            else:
+                scatter_piece(it, 1)
+        when(has[1], low_end)
 
         def update(p, it=it):
             n = ROWS[p][1]
@@ -469,10 +549,10 @@
             vm((NE, 3 * NE), BF16), vm((NE, 3 * NE), BF16), vm((2, 2, 2, NX, NX), BF16),
             vm((NR, NE, NX), F32), vm((2, 4, NY // 2 * NH, NX), BF16), vm((NY + 4 * my, NE, NX), F32),
             vm((ITERS, NR, NE, NX), F32), vm((ITERS, NR, NE, NX), F32),
-            vm((ITERS, 2, my, NE, NX), F32), vm((ITERS, 2, NY, HZ, NX), F32),
+            vm((ITERS, 2, my, NE, NX), F32), vm((ITERS, 2, NY, HZ, NX), F32), vm((ITERS, 2, my, HZ, NX), F32),
             pltpu.SemaphoreType.DMA((6,)), pltpu.SemaphoreType.DMA((5,)),
             pltpu.SemaphoreType.DMA((2, 2)), pltpu.SemaphoreType.DMA((2, 2)),
-            pltpu.SemaphoreType.DMA((2 * ITERS, 16)), pltpu.SemaphoreType.DMA((2 * ITERS, 16)),
+            pltpu.SemaphoreType.DMA((2 * ITERS, 20)), pltpu.SemaphoreType.DMA((2 * ITERS, 20)),
             pltpu.SemaphoreType.DMA((7,)), pltpu.SemaphoreType.DMA((7,)),
         ],
         compiler_params=pltpu.CompilerParams(

time: 42.7 us -> 39.1 us (0.916)
  the two profiles are of different devices: /device:TPU:19 before, /device:TPU:13 now
where the time goes in v2:
time: 39.1 us; the launch traced here: 39 us
  Pallas kernels  36.2 us (93%)
  local copies, waits for them, and re-layouts  2.81 us (7%)
    pallas_call x1, Pallas kernels, on_device(): pl.pallas_call(functools.partial(kernel, dims), out_shape=jax.ShapeDtypeS...  36.2 us
    transpose x1, local copies, waits for them, and re-layouts, on_device(): return jnp.transpose(out, (1, 0, 2))  2.81 us

profile of v2, /device:TPU:13, one launch (start us, length us, event | category | flops | bytes accessed | tf_op | source)
XLA Modules:
  0.0 39.0 jit_solution(1459904637340116290)
XLA Ops:
  0.0 36.2 %shard_map.55 = f32[16,64,256]{2,1,0:T(8,128)} custom-call(f32[1,64,16,256]{3,2,1,0:T(8,128)} %obs_hbm.1, f32[64,16,256]{2,1,0:T(8,128)} %start_hbm.1, f32[1,31]{1,0:T(1,128)} %sz_ref.1, f32[1,7]{1,0:T(1,128)} %sy_ref.1, f32[1,7]{1,0:T(1,128)} %sx_ref.1), custom_call_target="tpu_custom_call" | custom-call | tf_op jit(solution)/shard_map/pallas_call | solution.py:539
  36.2 2.8 %copy.6 = f32[64,16,256]{2,1,0:T(8,128)} copy(f32[64,16,256]{2,0,1:T(8,128)} %bitcast.1) | data formatting | bytes 2097152 | tf_op jit(solution)/shard_map/transpose | solution.py:561

commit v3 on v2

--- a/solution.py
+++ b/solution.py
@@ -540,7 +540,7 @@
         functools.partial(kernel, dims),
         out_shape=jax.ShapeDtypeStruct((NY, NZ, NX), F32),
         in_specs=[hbm] * 5,
-        out_specs=hbm,
+        out_specs=pl.BlockSpec(memory_space=pl.ANY),
         scratch_shapes=[
             vm((1, KZ), F32), vm((1, KY), F32), vm((1, KX), F32),
             vm((1, NH, NY, NX), F32), vm((2, HZ, NY, NX), F32),
@@ -556,8 +556,8 @@
             pltpu.SemaphoreType.DMA((7,)), pltpu.SemaphoreType.DMA((7,)),
         ],
         compiler_params=pltpu.CompilerParams(
-            collective_id=0, has_side_effects=True, vmem_limit_bytes=67043328),
-    )(observed, start, spread_z, spread_y, spread_x)
+            collective_id=0, has_side_effects=True, vmem_limit_bytes=24 << 20),
+    )(*(pltpu.with_memory_space_constraint(x, pltpu.HBM) for x in (observed, start, spread_z, spread_y, spread_x)))
     return jnp.transpose(out, (1, 0, 2))
 
 

time: 39.1 us -> 37.8 us (0.967)
  local copies, waits for them, and re-layouts: 2.81 us -> 1.58 us
    transpose x1, local copies, waits for them, and re-layouts: 2.81 us -> 1.58 us  [on_device(): return jnp.transpose(out, (1, 0, 2))]
where the time goes in v3:
time: 37.8 us; the launch traced here: 37.6 us
  Pallas kernels  36 us (95%)
  local copies, waits for them, and re-layouts  1.58 us (4%)
    pallas_call x1, Pallas kernels, on_device(): pl.pallas_call(functools.partial(kernel, dims), out_shape=jax.ShapeDtypeS...  36 us
    transpose x1, local copies, waits for them, and re-layouts, on_device(): return jnp.transpose(out, (1, 0, 2))  1.58 us

profile of v3, /device:TPU:13, one launch (start us, length us, event | category | flops | bytes accessed | tf_op | source)
XLA Modules:
  0.0 37.6 jit_solution(15272348404441791989)
XLA Ops:
  0.0 36.0 %shard_map.55 = f32[16,64,256]{2,1,0:T(8,128)S(1)} custom-call(f32[1,64,16,256]{3,2,1,0:T(8,128)} %obs_hbm.1, f32[64,16,256]{2,1,0:T(8,128)} %start_hbm.1, f32[1,31]{1,0:T(1,128)} %sz_ref.1, f32[1,7]{1,0:T(1,128)} %sy_ref.1, f32[1,7]{1,0:T(1,128)} %sx_ref.1), custom_call_target="tpu_custom_call" | custom-call | tf_op jit(solution)/shard_map/pallas_call | solution.py:539
  36.1 1.6 %copy.6 = f32[64,16,256]{2,1,0:T(8,128)} copy(f32[64,16,256]{2,0,1:T(8,128)S(1)} %bitcast.1) | data formatting | bytes 2097152 | tf_op jit(solution)/shard_map/transpose | solution.py:561

commit v4 on v3

--- a/solution.py
+++ b/solution.py
@@ -25,11 +25,11 @@
 
 def kernel(dims, obs_hbm, start_hbm, sz_ref, sy_ref, sx_ref, out_hbm,
            raw_z, raw_y, raw_x, stage, land, obs_z, obs_t, mine, theirs, wf, wb, tx, zbuf, ybuf, qbuf,
-           ebuf, cbuf, rybuf, rzbuf, sbuf, lsem, osem, gsem, hsem, ssem, rsem, xssem, xrsem):
+           ebuf, cbuf, rybuf, rzbuf, sbuf, lsem, ssem, rsem, xssem, xrsem):
     NH, NY, NX, HZ, KZ, KY, KX, S, G = dims
     my, mz, mx = KY // 2, KZ // 2, KX // 2
     NE, NR, NQ = NH + 2 * HZ, NY + 2 * my, NY + 4 * my
-    CH = NY // 2
+    CH, NP = NY // 2, 5
     v = lax.axis_index("view")
     gy = lax.axis_index("gy")
     s = 2 * lax.axis_index("gz") + v
@@ -76,7 +76,7 @@
     load_start.start()
     load_obs = pltpu.make_async_copy(obs_hbm.at[0, pl.ds(v * NH, NH)], obs_z.at[v], lsem.at[1])
     load_obs.start()
-    loads = [pltpu.make_async_copy(ref, raw, lsem.at[3 + k])
+    loads = [pltpu.make_async_copy(ref, raw, lsem.at[2 + k])
              for k, (ref, raw) in enumerate(((sz_ref, raw_z), (sy_ref, raw_y), (sx_ref, raw_x)))]
     for load in loads:
         load.start()
@@ -90,7 +90,7 @@
         return pltpu.make_async_remote_copy(
             src_ref=start_hbm.at[pl.ds(src0, mz), pl.ds(b0, CH)],
             dst_ref=land.at[d, pl.ds(dst0, mz), pl.ds(b0, CH)],
-            send_sem=gsem.at[d, k], recv_sem=hsem.at[d, k], device_id=zto[d], device_id_type=MESH)
+            send_sem=ssem.at[NP * d + k], recv_sem=rsem.at[NP * d + k], device_id=zto[d], device_id_type=MESH)
 
     peers = sum(there.astype(jnp.int32) for there, _ in greet)
     with scope("Wbar"):
@@ -112,14 +112,14 @@
             zbuf[pl.ds(row((my + NY, 0)[d], my), my)] = jnp.zeros((my, NE, NX), F32)
         when(jnp.logical_not(has[d]), blank_rows)
 
-    def copy(phase, m, src, dst, to):
+    def copy(send, recv, src, dst, to):
         return pltpu.make_async_remote_copy(
-            src_ref=src, dst_ref=dst, send_sem=ssem.at[phase, m], recv_sem=rsem.at[phase, m],
+            src_ref=src, dst_ref=dst, send_sem=ssem.at[send], recv_sem=rsem.at[recv],
             device_id=to, device_id_type=MESH)
 
     ROWS = ((NY, my), (my, my), (2 * my, NY - 4 * my), (NY - 2 * my, my), (NY - my, my))
     OUT, MID = NY - 3 * my, 2 * my
-    NP = len(ROWS)
+    assert len(ROWS) == NP
     ZED = ((HZ, NH), (0, HZ), (HZ + NH, HZ))
     zed_has = (None, dn_z, up_z)
     EDGE, HALO = (NY, my), (my + NY, 0)
@@ -130,54 +130,80 @@
         src0, dst0 = ((NH, 0), (HZ, HZ + NH))[d]
         n = ROWS[p][1]
         r0 = row(*ROWS[p])
-        return copy(2 * it, NP * d + p, e.at[pl.ds(r0, n), pl.ds(src0, HZ)],
+        return copy(NP * d + p, NP * d + p, e.at[pl.ds(r0, n), pl.ds(src0, HZ)],
                     e.at[pl.ds(r0, n), pl.ds(dst0, HZ)], zto[d])
 
     def gyc(it, d, p):
         e = ebuf.at[it]
         z0, n = ZED[p]
-        return copy(2 * it, 2 * NP + 3 * d + p, e.at[pl.ds(row(EDGE[d], my), my), pl.ds(z0, n)],
+        k = 2 * min(p, 1) + d
+        return copy(2 * NP + k, 4 * NP + k, e.at[pl.ds(row(EDGE[d], my), my), pl.ds(z0, n)],
                     e.at[pl.ds(THERE[d], my), pl.ds(z0, n)], yto[d])
 
     def fwd(it, d, q):
         rows_ = pl.ds(row(HALO[d], my), my)
         e = ebuf.at[it]
-        return copy(2 * it, 2 * NP + 6 + 2 * d + q, e.at[rows_, pl.ds((NH, HZ)[q], HZ)],
+        return copy(2 * NP + 4 + d, 4 * NP + 4 + d, e.at[rows_, pl.ds((NH, HZ)[q], HZ)],
                     e.at[rows_, pl.ds((0, HZ + NH)[q], HZ)], partner)
 
     def sfwd(it, d, q):
         rows_ = pl.ds(row(HALO[d], my), my)
-        return copy(2 * it + 1, 2 * NP + 6 + 2 * d + q, cbuf.at[it, rows_, pl.ds((HZ + NH, 0)[q], HZ)],
+        return copy(2 * NP + 4 + d, 4 * NP + 10 + d, cbuf.at[it, rows_, pl.ds((HZ + NH, 0)[q], HZ)],
                     sbuf.at[it, d], partner)
 
     def diagonal(it, d, q):
         z0, n = ZED[1 + q]
-        return copy(2 * it + 1, 2 * NP + 3 * d + 1 + q, cbuf.at[it, pl.ds(row(HALO[d], my), my), pl.ds(z0, n)],
+        return copy(2 * NP + 2 + d, 4 * NP + 8 + d, cbuf.at[it, pl.ds(row(HALO[d], my), my), pl.ds(z0, n)],
                     rybuf.at[it, d, :, pl.ds(0, HZ)], diag[d])
 
     def sz(it, d, p):
         src0 = (HZ + NH, 0)[d]
         n = ROWS[p][1]
         r0 = row(*ROWS[p])
-        return copy(2 * it + 1, NP * d + p, cbuf.at[it, pl.ds(r0, n), pl.ds(src0, HZ)],
+        return copy(NP * d + p, 2 * NP + NP * d + p, cbuf.at[it, pl.ds(r0, n), pl.ds(src0, HZ)],
                     rzbuf.at[it, d, pl.ds(r0 - my, n)], zto[d])
 
     def sy(it, d, p):
         z0, n = ZED[p]
-        return copy(2 * it + 1, 2 * NP + 3 * d + p, cbuf.at[it, pl.ds(row(HALO[d], my), my), pl.ds(z0, n)],
+        k = 2 * min(p, 1) + d
+        return copy(2 * NP + k, 4 * NP + 6 + k, cbuf.at[it, pl.ds(row(HALO[d], my), my), pl.ds(z0, n)],
                     rybuf.at[it, d, :, pl.ds(z0, n)], yto[d])
 
+    def follow(before, now):
+        if before is not None:
+            before.wait_send()
+        now.start()
+
+    def send_gz(it, d, p):
+        follow(sz(it - 1, d, p), gz(it, d, p))
+
+    def send_sz(it, d, p):
+        follow(gz(it, d, p) if it > 0 else first(d, p) if p < 2 else None, sz(it, d, p))
+
+    def send_gy(it, d, p):
+        follow(sy(it - 1, d, p) if it > 0 else None, gyc(it, d, p))
+
+    def send_sy(it, d, p):
+        now = diagonal(it, d, p - 1) if p > 0 and it + 1 == ITERS else sy(it, d, p)
+        follow(gyc(it, d, p), now)
+
+    def send_fwd(it, d, q):
+        follow(sfwd(it - 1, d, q) if it > 0 else None, fwd(it, d, q))
+
+    def send_sfwd(it, d, q):
+        follow(fwd(it, d, q), sfwd(it, d, q))
+
     def gather_piece(it, p):
         for d in range(2):
-            when(zhas[d], gz(it, d, p).start)
+            when(zhas[d], functools.partial(send_gz, it, d, p))
 
     def gather_own(it):
         for d in range(2):
-            when(has[d], gyc(it, d, 0).start)
+            when(has[d], functools.partial(send_gy, it, d, 0))
 
     def relay(it, p, d):
         if p < 2:
-            when(both(both(zfrom[d], has[p]), v == d), gyc(it, p, 1 + d).start)
+            when(both(both(zfrom[d], has[p]), v == d), functools.partial(send_gy, it, p, 1 + d))
 
     def gather_take(it, p):
         for d in range(2):
@@ -199,7 +225,7 @@
         def go():
             gyc(it, d, 0).wait_recv()
             for q in range(2):
-                when(v == q, fwd(it, d, q).start)
+                when(v == q, functools.partial(send_fwd, it, d, q))
         when(has[d], go)
 
     def gather_edge(it, d):
@@ -207,26 +233,25 @@
             when(both(both(zed_has[1 + q], has[d]), v == q), gyc(it, d, 1 + q).wait_recv)
             when(both(has[d], v == 1 - q), fwd(it, d, q).wait_recv)
 
-    def sent(it):
-        for d in range(2):
-            for p in range(NP):
-                if it > 0:
-                    when(zhas[d], gz(it, d, p).wait_send)
-                when(zhas[d], sz(it, d, p).wait_send)
-            for y in (gyc, sy):
-                when(has[d], y(it, d, 0).wait_send)
+    def sent():
+        it = ITERS - 1
+        for d in range(2):
+            def along_z(d=d):
+                for p in range(NP):
+                    sz(it, d, p).wait_send()
+            when(zhas[d], along_z)
+
+            def along_y(d=d):
+                sy(it, d, 0).wait_send()
                 for q in range(2):
-                    corner = diagonal(it, d, q) if y is sy and it + 1 == ITERS else y(it, d, 1 + q)
-                    when(both(both(zed_has[1 + q], has[d]), v == q), corner.wait_send)
-            for y in (fwd, sfwd):
-                for q in range(2):
-                    when(both(has[d], v == q), y(it, d, q).wait_send)
+                    when(both(zed_has[1 + q], v == q), diagonal(it, d, q).wait_send)
+                    when(v == q, sfwd(it, d, q).wait_send)
+            when(has[d], along_y)
 
     def scatter_edge(it, d):
         for q in range(2):
-            corner = diagonal(it, d, q) if it + 1 == ITERS else sy(it, d, 1 + q)
-            when(both(both(zed_has[1 + q], has[d]), v == q), corner.start)
-            when(both(has[d], v == q), sfwd(it, d, q).start)
+            when(both(both(zed_has[1 + q], has[d]), v == q), functools.partial(send_sy, it, d, 1 + q))
+            when(both(has[d], v == q), functools.partial(send_sfwd, it, d, q))
 
     def scatter_own(it, d):
         r0 = row(HALO[d], my)
@@ -236,11 +261,11 @@
                 sfwd(it, d, q).wait_recv()
                 cbuf[it, pl.ds(r0, my), z0:z0 + HZ, :] += sbuf[it, d]
             when(both(has[d], v == 1 - q), add)
-        when(has[d], sy(it, d, 0).start)
+        when(has[d], functools.partial(send_sy, it, d, 0))
 
     def scatter_piece(it, p):
         for d in range(2):
-            when(zhas[d], sz(it, d, p).start)
+            when(zhas[d], functools.partial(send_sz, it, d, p))
 
     def scatter_end(it, p):
         r0 = row(*ROWS[p])
@@ -251,11 +276,11 @@
                 sy(it, p, 1 + q).wait_recv()
                 cbuf[it, pl.ds(r0, my), z0:z0 + HZ, :] += rybuf[it, p, :, z0:z0 + HZ, :]
             when(both(both(zed_has[1 + q], has[p]), v == q), add)
-            when(both(zed_has[1 + q], v == q), sz(it, 1 - q, p).start)
+            when(both(zed_has[1 + q], v == q), functools.partial(send_sz, it, 1 - q, p))
 
     def scatter_near(it, p):
         for q in range(2):
-            when(v == 1 - q, sz(it, 1 - q, p).start)
+            when(v == 1 - q, functools.partial(send_sz, it, 1 - q, p))
 
     def scatter_take(it, p):
         n = ROWS[p][1]
@@ -481,7 +506,6 @@
             else:
                 scatter_piece(it, 1)
         when(has[1], low_end)
-
         def update(p, it=it):
             n = ROWS[p][1]
             r0 = row(*ROWS[p])
@@ -504,26 +528,23 @@
             gather_piece(it + 1, 4)
         else:
             outs = []
-            for n, p in enumerate((1, 2, 3, 4, 0)):
-                update(p)
-                r0 = row(*ROWS[p])
-                rows_ = ROWS[p][1]
+            for n, (pieces, i0, rows_) in enumerate((((1, 2, 3), my, NY - 2 * my), ((4, 0), NY - my, 2 * my))):
+                for p in pieces:
+                    update(p)
+                r0 = row(i0, rows_)
                 src = zbuf.at[pl.ds(r0, rows_), pl.ds(0, NH)]
                 dst = out_hbm.at[pl.ds(r0 - my, rows_), pl.ds(v * NH, NH)]
-                outs.append(pltpu.make_async_copy(src, dst, osem.at[n]))
+                outs.append(pltpu.make_async_copy(src, dst, lsem.at[n]))
                 outs.append(pltpu.make_async_remote_copy(
-                    src_ref=src, dst_ref=dst, send_sem=xssem.at[2 + n], recv_sem=xrsem.at[2 + n],
+                    src_ref=src, dst_ref=dst, send_sem=xssem.at[n], recv_sem=xrsem.at[n],
                     device_id=partner, device_id_type=MESH))
                 outs[-1].start()
                 outs[-2].start()
+            with scope("Wsent2"):
+                sent()
             with scope("Wout"):
                 for out in outs:
                     out.wait()
-    for it in range(ITERS):
-        sent(it)
-    for k in range(2):
-        for d in range(2):
-            when(zhas[d], first(d, k).wait_send)
 
 
 def on_device(S, G, observed, start, spread_z, spread_y, spread_x):
@@ -550,10 +571,8 @@
             vm((NR, NE, NX), F32), vm((2, 4, NY // 2 * NH, NX), BF16), vm((NY + 4 * my, NE, NX), F32),
             vm((ITERS, NR, NE, NX), F32), vm((ITERS, NR, NE, NX), F32),
             vm((ITERS, 2, my, NE, NX), F32), vm((ITERS, 2, NY, HZ, NX), F32), vm((ITERS, 2, my, HZ, NX), F32),
-            pltpu.SemaphoreType.DMA((6,)), pltpu.SemaphoreType.DMA((5,)),
-            pltpu.SemaphoreType.DMA((2, 2)), pltpu.SemaphoreType.DMA((2, 2)),
-            pltpu.SemaphoreType.DMA((2 * ITERS, 20)), pltpu.SemaphoreType.DMA((2 * ITERS, 20)),
-            pltpu.SemaphoreType.DMA((7,)), pltpu.SemaphoreType.DMA((7,)),
+            pltpu.SemaphoreType.DMA((5,)), pltpu.SemaphoreType.DMA((16,)), pltpu.SemaphoreType.DMA((32,)),
+            pltpu.SemaphoreType.DMA((2,)), pltpu.SemaphoreType.DMA((2,)),
         ],
         compiler_params=pltpu.CompilerParams(
             collective_id=0, has_side_effects=True, vmem_limit_bytes=24 << 20),

time: 37.8 us -> 36.9 us (0.976)
  Pallas kernels: 36 us -> 34.9 us
    pallas_call x1, Pallas kernels: 36 us -> 34.9 us  [on_device(): pl.pallas_call(functools.partial(kernel, dims), out_shape=jax.ShapeDtypeS...]
where the time goes in v4:
time: 36.9 us; the launch traced here: 36.5 us
  Pallas kernels  34.9 us (95%)
  local copies, waits for them, and re-layouts  1.58 us (4%)
    pallas_call x1, Pallas kernels, on_device(): pl.pallas_call(functools.partial(kernel, dims), out_shape=jax.ShapeDtypeS...  34.9 us
    transpose x1, local copies, waits for them, and re-layouts, on_device(): return jnp.transpose(out, (1, 0, 2))  1.58 us

profile of v4, /device:TPU:13, one launch (start us, length us, event | category | flops | bytes accessed | tf_op | source)
XLA Modules:
  0.0 36.5 jit_solution(9149309590053529017)
XLA Ops:
  0.0 34.9 %shard_map.55 = f32[16,64,256]{2,1,0:T(8,128)S(1)} custom-call(f32[1,64,16,256]{3,2,1,0:T(8,128)} %obs_hbm.1, f32[64,16,256]{2,1,0:T(8,128)} %start_hbm.1, f32[1,31]{1,0:T(1,128)} %sz_ref.1, f32[1,7]{1,0:T(1,128)} %sy_ref.1, f32[1,7]{1,0:T(1,128)} %sx_ref.1), custom_call_target="tpu_custom_call" | custom-call | tf_op jit(solution)/shard_map/pallas_call | solution.py:560
  34.9 1.6 %copy.6 = f32[64,16,256]{2,1,0:T(8,128)} copy(f32[64,16,256]{2,0,1:T(8,128)S(1)} %bitcast.1) | data formatting | bytes 2097152 | tf_op jit(solution)/shard_map/transpose | solution.py:580

commit v5 on v4

--- a/solution.py
+++ b/solution.py
@@ -29,7 +29,7 @@
     NH, NY, NX, HZ, KZ, KY, KX, S, G = dims
     my, mz, mx = KY // 2, KZ // 2, KX // 2
     NE, NR, NQ = NH + 2 * HZ, NY + 2 * my, NY + 4 * my
-    CH, NP = NY // 2, 5
+    CH, NP = NY // 2, 4
     v = lax.axis_index("view")
     gy = lax.axis_index("gy")
     s = 2 * lax.axis_index("gz") + v
@@ -117,7 +117,7 @@
             src_ref=src, dst_ref=dst, send_sem=ssem.at[send], recv_sem=rsem.at[recv],
             device_id=to, device_id_type=MESH)
 
-    ROWS = ((NY, my), (my, my), (2 * my, NY - 4 * my), (NY - 2 * my, my), (NY - my, my))
+    ROWS = ((NY, my), (my, my), (2 * my, NY - 3 * my), (NY - my, my))
     OUT, MID = NY - 3 * my, 2 * my
     assert len(ROWS) == NP
     ZED = ((HZ, NH), (0, HZ), (HZ + NH, HZ))
@@ -434,7 +434,7 @@
                 first_take(1)
             zrows(my, CH)
         else:
-            for p in (1, 2, 3):
+            for p in (1, 2):
                 with scope(f"Wg{it}_{p}"):
                     gather_take(it, p)
                 zrows(*ROWS[p])
@@ -463,15 +463,13 @@
         when(jnp.logical_not(has[1]), functools.partial(scatter_piece, it, 1))
         if it == 0:
             qrows(OUT, MID)
-            for p in (2, 3):
-                crows(*ROWS[p])
-                scatter_piece(it, p)
+            crows(*ROWS[2])
+            scatter_piece(it, 2)
             when(has[0], high_edge)
             qrows(OUT + MID, my)
             when(has[0], high_scatter)
-            crows(*ROWS[4])
-            scatter_piece(it, 4)
-            crows(*ROWS[0])
+            crows(NY - my, 2 * my)
+            scatter_piece(it, 3)
             scatter_near(it, 0)
             with scope(f"Wse{it}"):
                 scatter_end(it, 0)
@@ -479,22 +477,20 @@
         else:
             with scope(f"Wg{it}_0"):
                 gather_take(it, 0)
-            zrows(*ROWS[0])
             with scope(f"Wge{it}own"):
                 edge_own(it, 0)
-            with scope(f"Wg{it}_4"):
-                gather_take(it, 4)
-            zrows(*ROWS[4])
+            with scope(f"Wg{it}_3"):
+                gather_take(it, 3)
+            zrows(NY - my, 2 * my)
             qrows(OUT, MID)
-            for p in (2, 3):
-                crows(*ROWS[p])
-                scatter_piece(it, p)
+            crows(*ROWS[2])
+            scatter_piece(it, 2)
             when(has[0], high_edge)
             qrows(OUT + MID, my)
             when(has[0], high_scatter)
-            for p in (0, 4):
-                crows(*ROWS[p])
-                scatter_piece(it, p)
+            crows(NY - my, 2 * my)
+            scatter_piece(it, 0)
+            scatter_piece(it, 3)
             with scope(f"Wso{it}"):
                 scatter_own(it, 0)
 
@@ -518,25 +514,26 @@
                 zbuf[pl.ds(r0, n), 0:NH, :] = new
 
         if it + 1 < ITERS:
-            for p in (1, 2, 3):
+            for p in (1, 2):
                 update(p)
                 gather_piece(it + 1, p)
             update(0)
             gather_piece(it + 1, 0)
             gather_own(it + 1)
-            update(4)
-            gather_piece(it + 1, 4)
+            update(3)
+            gather_piece(it + 1, 3)
         else:
             outs = []
-            for n, (pieces, i0, rows_) in enumerate((((1, 2, 3), my, NY - 2 * my), ((4, 0), NY - my, 2 * my))):
+            for k, pieces in enumerate(((1, 2), (3, 0))):
                 for p in pieces:
                     update(p)
-                r0 = row(i0, rows_)
-                src = zbuf.at[pl.ds(r0, rows_), pl.ds(0, NH)]
-                dst = out_hbm.at[pl.ds(r0 - my, rows_), pl.ds(v * NH, NH)]
-                outs.append(pltpu.make_async_copy(src, dst, lsem.at[n]))
+                b0 = pl.multiple_of(blocks[1 - k], CH)
+                stage[0, :, pl.ds(b0, CH), :] = jnp.transpose(zbuf[pl.ds(my + b0, CH), 0:NH, :], (1, 0, 2))
+                src = stage.at[0, :, pl.ds(b0, CH)]
+                dst = out_hbm.at[pl.ds(v * NH, NH), pl.ds(b0, CH)]
+                outs.append(pltpu.make_async_copy(src, dst, lsem.at[k]))
                 outs.append(pltpu.make_async_remote_copy(
-                    src_ref=src, dst_ref=dst, send_sem=xssem.at[n], recv_sem=xrsem.at[n],
+                    src_ref=src, dst_ref=dst, send_sem=xssem.at[k], recv_sem=xrsem.at[k],
                     device_id=partner, device_id_type=MESH))
                 outs[-1].start()
                 outs[-2].start()
@@ -545,6 +542,12 @@
             with scope("Wout"):
                 for out in outs:
                     out.wait()
+
+
+def store(src, dst, sem):
+    copy = pltpu.make_async_copy(src, dst, sem)
+    copy.start()
+    copy.wait()
 
 
 def on_device(S, G, observed, start, spread_z, spread_y, spread_x):
@@ -559,7 +562,7 @@
     hbm = pl.BlockSpec(memory_space=pltpu.HBM)
     out = pl.pallas_call(
         functools.partial(kernel, dims),
-        out_shape=jax.ShapeDtypeStruct((NY, NZ, NX), F32),
+        out_shape=jax.ShapeDtypeStruct((NZ, NY, NX), F32),
         in_specs=[hbm] * 5,
         out_specs=pl.BlockSpec(memory_space=pl.ANY),
         scratch_shapes=[
@@ -571,13 +574,20 @@
             vm((NR, NE, NX), F32), vm((2, 4, NY // 2 * NH, NX), BF16), vm((NY + 4 * my, NE, NX), F32),
             vm((ITERS, NR, NE, NX), F32), vm((ITERS, NR, NE, NX), F32),
             vm((ITERS, 2, my, NE, NX), F32), vm((ITERS, 2, NY, HZ, NX), F32), vm((ITERS, 2, my, HZ, NX), F32),
-            pltpu.SemaphoreType.DMA((5,)), pltpu.SemaphoreType.DMA((16,)), pltpu.SemaphoreType.DMA((32,)),
+            pltpu.SemaphoreType.DMA((5,)), pltpu.SemaphoreType.DMA((14,)), pltpu.SemaphoreType.DMA((28,)),
             pltpu.SemaphoreType.DMA((2,)), pltpu.SemaphoreType.DMA((2,)),
         ],
         compiler_params=pltpu.CompilerParams(
             collective_id=0, has_side_effects=True, vmem_limit_bytes=24 << 20),
     )(*(pltpu.with_memory_space_constraint(x, pltpu.HBM) for x in (observed, start, spread_z, spread_y, spread_x)))
-    return jnp.transpose(out, (1, 0, 2))
+    return pl.pallas_call(
+        store,
+        out_shape=jax.ShapeDtypeStruct((NZ, NY, NX), F32),
+        in_specs=[pl.BlockSpec(memory_space=pl.ANY)],
+        out_specs=hbm,
+        scratch_shapes=[pltpu.SemaphoreType.DMA],
+        compiler_params=pltpu.CompilerParams(vmem_limit_bytes=4 << 20),
+    )(out)
 
 
 def solution(mesh):

time: 36.9 us -> 36.3 us (0.984)
  local copies, waits for them, and re-layouts: 1.58 us -> 0 us
  Pallas kernels: 34.9 us -> 35.8 us
    transpose x1 -> x0, local copies, waits for them, and re-layouts: 1.58 us -> none  [on_device(): return jnp.transpose(out, (1, 0, 2))]
    pallas_call x0 -> x1, Pallas kernels: none -> 0.98 us  [on_device(): pl.pallas_call(store, out_shape=jax.ShapeDtypeStruct((NZ, NY, NX), F32),...]
where the time goes in v5:
time: 36.3 us; the launch traced here: 35.8 us
  Pallas kernels  35.8 us (99%)
    pallas_call x1, Pallas kernels, on_device(): pl.pallas_call(functools.partial(kernel, dims), out_shape=jax.ShapeDtypeS...  34.8 us
    pallas_call x1, Pallas kernels, on_device(): pl.pallas_call(store, out_shape=jax.ShapeDtypeStruct((NZ, NY, NX), F32),...  0.98 us

profile of v5, /device:TPU:13, one launch (start us, length us, event | category | flops | bytes accessed | tf_op | source)
XLA Modules:
  0.0 35.8 jit_solution(17312280314943165818)
XLA Ops:
  0.0 34.8 %shard_map.55.src = f32[64,16,256]{2,1,0:T(8,128)S(1)} custom-call(f32[1,64,16,256]{3,2,1,0:T(8,128)} %obs_hbm.1, f32[64,16,256]{2,1,0:T(8,128)} %start_hbm.1, f32[1,31]{1,0:T(1,128)} %sz_ref.1, f32[1,7]{1,0:T(1,128)} %sy_ref.1, f32[1,7]{1,0:T(1,128)} %sx_ref.1), custom_call_target="tpu_custom_call" | custom-call | tf_op jit(solution)/shard_map/pallas_call | solution.py:563
  34.8 1.0 %shard_map.56 = f32[64,16,256]{2,1,0:T(8,128)} custom-call(f32[64,16,256]{2,1,0:T(8,128)S(1)} %shard_map.55.src), custom_call_target="tpu_custom_call" | custom-call | tf_op jit(solution)/shard_map/pallas_call | solution.py:583

commit v6 on v5

--- a/solution.py
+++ b/solution.py
@@ -29,7 +29,7 @@
     NH, NY, NX, HZ, KZ, KY, KX, S, G = dims
     my, mz, mx = KY // 2, KZ // 2, KX // 2
     NE, NR, NQ = NH + 2 * HZ, NY + 2 * my, NY + 4 * my
-    CH, NP = NY // 2, 4
+    CH, NP = NY // 2, 5
     v = lax.axis_index("view")
     gy = lax.axis_index("gy")
     s = 2 * lax.axis_index("gz") + v
@@ -117,7 +117,7 @@
             src_ref=src, dst_ref=dst, send_sem=ssem.at[send], recv_sem=rsem.at[recv],
             device_id=to, device_id_type=MESH)
 
-    ROWS = ((NY, my), (my, my), (2 * my, NY - 3 * my), (NY - my, my))
+    ROWS = ((NY, my), (my, my + 1), (2 * my + 1, NY - 4 * my - 1), (NY - 2 * my, my), (NY - my, my))
     OUT, MID = NY - 3 * my, 2 * my
     assert len(ROWS) == NP
     ZED = ((HZ, NH), (0, HZ), (HZ + NH, HZ))
@@ -268,7 +268,7 @@
             when(zhas[d], functools.partial(send_sz, it, d, p))
 
     def scatter_end(it, p):
-        r0 = row(*ROWS[p])
+        r0 = row(EDGE[p], my)
         for q in range(2):
             z0 = ZED[1 + q][0]
 
@@ -288,14 +288,14 @@
         if p < 2:
             def add_y():
                 sy(it, p, 0).wait_recv()
-                cbuf[it, pl.ds(r0, n), HZ:HZ + NH, :] += rybuf[it, p, :, HZ:HZ + NH, :]
+                cbuf[it, pl.ds(row(EDGE[p], my), my), HZ:HZ + NH, :] += rybuf[it, p, :, HZ:HZ + NH, :]
             when(has[p], add_y)
             if it + 1 == ITERS:
                 for q in range(2):
                     def add_diagonal(q=q):
                         z0 = (NH, HZ)[q]
                         diagonal(it, p, q).wait_recv()
-                        cbuf[it, pl.ds(r0, n), z0:z0 + HZ, :] += rybuf[it, p, :, 0:HZ, :]
+                        cbuf[it, pl.ds(row(EDGE[p], my), my), z0:z0 + HZ, :] += rybuf[it, p, :, 0:HZ, :]
                     when(both(both(zed_has[2 - q], has[p]), v == 1 - q), add_diagonal)
         for d in range(2):
             z0 = (HZ, NH)[d]
@@ -424,6 +424,10 @@
                     cbuf[it, r] = jnp.dot(wb[...], stacked(jnp.concatenate(parts, axis=0)),
                                           preferred_element_type=F32)
 
+        def low_edge(it=it):
+            edge_own(it, 1)
+            gather_edge(it, 1)
+            zrows(0, my)
         if it == 0:
             with scope("Wg0_in"):
                 first_take(0)
@@ -433,17 +437,20 @@
             with scope("Wg0_out"):
                 first_take(1)
             zrows(my, CH)
+            when(has[1], low_edge)
+            qrows(0, OUT)
         else:
             for p in (1, 2):
                 with scope(f"Wg{it}_{p}"):
                     gather_take(it, p)
                 zrows(*ROWS[p])
-
-        def low_edge(it=it):
-            edge_own(it, 1)
-            gather_edge(it, 1)
-            zrows(0, my)
-        when(has[1], low_edge)
+            when(has[1], low_edge)
+            qrows(0, my + 1)
+            with scope(f"Wg{it}_3"):
+                gather_take(it, 3)
+            zrows(*ROWS[3])
+            qrows(my + 1, OUT - my - 1)
+
         def low_scatter(it=it):
             crows(0, my)
             scatter_edge(it, 1)
@@ -457,19 +464,19 @@
             crows(my + NY, my)
             scatter_edge(it, 0)
 
-        qrows(0, OUT)
         when(has[1], low_scatter)
         crows(*ROWS[1])
         when(jnp.logical_not(has[1]), functools.partial(scatter_piece, it, 1))
         if it == 0:
             qrows(OUT, MID)
-            crows(*ROWS[2])
+            crows(2 * my + 1, NY - 3 * my - 1)
             scatter_piece(it, 2)
+            scatter_piece(it, 3)
             when(has[0], high_edge)
             qrows(OUT + MID, my)
             when(has[0], high_scatter)
             crows(NY - my, 2 * my)
-            scatter_piece(it, 3)
+            scatter_piece(it, 4)
             scatter_near(it, 0)
             with scope(f"Wse{it}"):
                 scatter_end(it, 0)
@@ -479,18 +486,19 @@
                 gather_take(it, 0)
             with scope(f"Wge{it}own"):
                 edge_own(it, 0)
-            with scope(f"Wg{it}_3"):
-                gather_take(it, 3)
+            with scope(f"Wg{it}_4"):
+                gather_take(it, 4)
             zrows(NY - my, 2 * my)
             qrows(OUT, MID)
-            crows(*ROWS[2])
+            crows(2 * my + 1, NY - 3 * my - 1)
             scatter_piece(it, 2)
+            scatter_piece(it, 3)
             when(has[0], high_edge)
             qrows(OUT + MID, my)
             when(has[0], high_scatter)
             crows(NY - my, 2 * my)
             scatter_piece(it, 0)
-            scatter_piece(it, 3)
+            scatter_piece(it, 4)
             with scope(f"Wso{it}"):
                 scatter_own(it, 0)
 
@@ -514,17 +522,17 @@
                 zbuf[pl.ds(r0, n), 0:NH, :] = new
 
         if it + 1 < ITERS:
-            for p in (1, 2):
+            for p in (1, 2, 3):
                 update(p)
                 gather_piece(it + 1, p)
             update(0)
             gather_piece(it + 1, 0)
             gather_own(it + 1)
-            update(3)
-            gather_piece(it + 1, 3)
+            update(4)
+            gather_piece(it + 1, 4)
         else:
             outs = []
-            for k, pieces in enumerate(((1, 2), (3, 0))):
+            for k, pieces in enumerate(((1, 2, 3), (4, 0))):
                 for p in pieces:
                     update(p)
                 b0 = pl.multiple_of(blocks[1 - k], CH)
@@ -574,7 +582,7 @@
             vm((NR, NE, NX), F32), vm((2, 4, NY // 2 * NH, NX), BF16), vm((NY + 4 * my, NE, NX), F32),
             vm((ITERS, NR, NE, NX), F32), vm((ITERS, NR, NE, NX), F32),
             vm((ITERS, 2, my, NE, NX), F32), vm((ITERS, 2, NY, HZ, NX), F32), vm((ITERS, 2, my, HZ, NX), F32),
-            pltpu.SemaphoreType.DMA((5,)), pltpu.SemaphoreType.DMA((14,)), pltpu.SemaphoreType.DMA((28,)),
+            pltpu.SemaphoreType.DMA((5,)), pltpu.SemaphoreType.DMA((16,)), pltpu.SemaphoreType.DMA((32,)),
             pltpu.SemaphoreType.DMA((2,)), pltpu.SemaphoreType.DMA((2,)),
         ],
         compiler_params=pltpu.CompilerParams(

time: 36.3 us -> 35.7 us (0.983); the launches traced: 35.8 us -> 35.6 us
  no operation moved by 1% of the time
where the time goes in v6:
time: 35.7 us; the launch traced here: 35.6 us
  Pallas kernels  35.6 us (100%)
    pallas_call x1, Pallas kernels, on_device(): pl.pallas_call(functools.partial(kernel, dims), out_shape=jax.ShapeDtypeS...  34.6 us
    pallas_call x1, Pallas kernels, on_device(): pl.pallas_call(store, out_shape=jax.ShapeDtypeStruct((NZ, NY, NX), F32),...  0.98 us

profile of v6, /device:TPU:13, one launch (start us, length us, event | category | flops | bytes accessed | tf_op | source)
XLA Modules:
  0.0 35.6 jit_solution(18286899397292661807)
XLA Ops:
  0.0 34.6 %shard_map.55.src = f32[64,16,256]{2,1,0:T(8,128)S(1)} custom-call(f32[1,64,16,256]{3,2,1,0:T(8,128)} %obs_hbm.1, f32[64,16,256]{2,1,0:T(8,128)} %start_hbm.1, f32[1,31]{1,0:T(1,128)} %sz_ref.1, f32[1,7]{1,0:T(1,128)} %sy_ref.1, f32[1,7]{1,0:T(1,128)} %sx_ref.1), custom_call_target="tpu_custom_call" | custom-call | tf_op jit(solution)/shard_map/pallas_call | solution.py:571
  34.6 1.0 %shard_map.56 = f32[64,16,256]{2,1,0:T(8,128)} custom-call(f32[64,16,256]{2,1,0:T(8,128)S(1)} %shard_map.55.src), custom_call_target="tpu_custom_call" | custom-call | tf_op jit(solution)/shard_map/pallas_call | solution.py:591

commit v7 on v6

--- a/solution.py
+++ b/solution.py
@@ -30,6 +30,7 @@
     my, mz, mx = KY // 2, KZ // 2, KX // 2
     NE, NR, NQ = NH + 2 * HZ, NY + 2 * my, NY + 4 * my
     CH, NP = NY // 2, 5
+    assert NH >= 2 * HZ
     v = lax.axis_index("view")
     gy = lax.axis_index("gy")
     s = 2 * lax.axis_index("gz") + v
@@ -140,6 +141,14 @@
         return copy(2 * NP + k, 4 * NP + k, e.at[pl.ds(row(EDGE[d], my), my), pl.ds(z0, n)],
                     e.at[pl.ds(THERE[d], my), pl.ds(z0, n)], yto[d])
 
+    HH = NH // 2
+
+    def sy_own(it, d, near):
+        z0 = pl.multiple_of(HZ + HH * (1 - v if near else v), 8)
+        return copy(2 * NP + (6 + d if near else d), 4 * NP + 6 + (6 + d if near else d),
+                    cbuf.at[it, pl.ds(row(HALO[d], my), my), pl.ds(z0, HH)],
+                    rybuf.at[it, d, :, pl.ds(z0, HH)], yto[d])
+
     def fwd(it, d, q):
         rows_ = pl.ds(row(HALO[d], my), my)
         e = ebuf.at[it]
@@ -181,7 +190,14 @@
         follow(gz(it, d, p) if it > 0 else first(d, p) if p < 2 else None, sz(it, d, p))
 
     def send_gy(it, d, p):
-        follow(sy(it - 1, d, p) if it > 0 else None, gyc(it, d, p))
+        before = None if it == 0 else sy_own(it - 1, d, False) if p == 0 else sy(it - 1, d, p)
+        follow(before, gyc(it, d, p))
+
+    def send_far(it, d):
+        follow(gyc(it, d, 0), sy_own(it, d, False))
+
+    def send_near(it, d):
+        follow(sy_own(it - 1, d, True) if it > 0 else None, sy_own(it, d, True))
 
     def send_sy(it, d, p):
         now = diagonal(it, d, p - 1) if p > 0 and it + 1 == ITERS else sy(it, d, p)
@@ -242,7 +258,8 @@
             when(zhas[d], along_z)
 
             def along_y(d=d):
-                sy(it, d, 0).wait_send()
+                sy_own(it, d, False).wait_send()
+                sy_own(it, d, True).wait_send()
                 for q in range(2):
                     when(both(zed_has[1 + q], v == q), diagonal(it, d, q).wait_send)
                     when(v == q, sfwd(it, d, q).wait_send)
@@ -252,6 +269,7 @@
         for q in range(2):
             when(both(both(zed_has[1 + q], has[d]), v == q), functools.partial(send_sy, it, d, 1 + q))
             when(both(has[d], v == q), functools.partial(send_sfwd, it, d, q))
+        when(has[d], functools.partial(send_far, it, d))
 
     def scatter_own(it, d):
         r0 = row(HALO[d], my)
@@ -261,7 +279,7 @@
                 sfwd(it, d, q).wait_recv()
                 cbuf[it, pl.ds(r0, my), z0:z0 + HZ, :] += sbuf[it, d]
             when(both(has[d], v == 1 - q), add)
-        when(has[d], functools.partial(send_sy, it, d, 0))
+        when(has[d], functools.partial(send_near, it, d))
 
     def scatter_piece(it, p):
         for d in range(2):
@@ -287,7 +305,8 @@
         r0 = row(*ROWS[p])
         if p < 2:
             def add_y():
-                sy(it, p, 0).wait_recv()
+                sy_own(it, p, False).wait_recv()
+                sy_own(it, p, True).wait_recv()
                 cbuf[it, pl.ds(row(EDGE[p], my), my), HZ:HZ + NH, :] += rybuf[it, p, :, HZ:HZ + NH, :]
             when(has[p], add_y)
             if it + 1 == ITERS:
@@ -478,9 +497,10 @@
             crows(NY - my, 2 * my)
             scatter_piece(it, 4)
             scatter_near(it, 0)
+            with scope(f"Wso{it}"):
+                scatter_own(it, 0)
             with scope(f"Wse{it}"):
                 scatter_end(it, 0)
-            scatter_own(it, 0)
         else:
             with scope(f"Wg{it}_0"):
                 gather_take(it, 0)
@@ -532,19 +552,59 @@
             gather_piece(it + 1, 4)
         else:
             outs = []
-            for k, pieces in enumerate(((1, 2, 3), (4, 0))):
-                for p in pieces:
-                    update(p)
-                b0 = pl.multiple_of(blocks[1 - k], CH)
-                stage[0, :, pl.ds(b0, CH), :] = jnp.transpose(zbuf[pl.ds(my + b0, CH), 0:NH, :], (1, 0, 2))
-                src = stage.at[0, :, pl.ds(b0, CH)]
-                dst = out_hbm.at[pl.ds(v * NH, NH), pl.ds(b0, CH)]
-                outs.append(pltpu.make_async_copy(src, dst, lsem.at[k]))
+            def leave(k, h, count):
+                b0 = pl.multiple_of(blocks[k], CH)
+                stage[0, pl.ds(h, count), pl.ds(b0, CH), :] = jnp.transpose(
+                    zbuf[pl.ds(my + b0, CH), pl.ds(h, count), :], (1, 0, 2))
+                src = stage.at[0, pl.ds(h, count), pl.ds(b0, CH)]
+                dst = out_hbm.at[pl.ds(v * NH + h, count), pl.ds(b0, CH)]
+                n = len(outs) // 2
+                outs.append(pltpu.make_async_copy(src, dst, lsem.at[n]))
                 outs.append(pltpu.make_async_remote_copy(
-                    src_ref=src, dst_ref=dst, send_sem=xssem.at[k], recv_sem=xrsem.at[k],
+                    src_ref=src, dst_ref=dst, send_sem=xssem.at[n], recv_sem=xrsem.at[n],
                     device_id=partner, device_id_type=MESH))
                 outs[-1].start()
                 outs[-2].start()
+
+            def finish(p, near):
+                n = ROWS[p][1]
+                r0 = row(*ROWS[p])
+                for q in range(2):
+                    def half(q=q):
+                        z0, h0 = (HZ, NH)[q], q * HH
+
+                        def add():
+                            sz(it, q, p).wait_recv()
+                            cbuf[it, pl.ds(r0, n), z0:z0 + HZ, :] += rzbuf[it, q, pl.ds(r0 - my, n)]
+                        when(zfrom[q], add)
+                        if p == 0 and not near:
+                            def add_diagonal():
+                                diagonal(it, p, 1 - q).wait_recv()
+                                cbuf[it, pl.ds(row(EDGE[p], my), my), z0:z0 + HZ, :] += rybuf[it, p, :, 0:HZ, :]
+                            when(both(zfrom[q], has[p]), add_diagonal)
+                        zbuf[pl.ds(r0, n), h0:h0 + HH, :] = (
+                            ebuf[it, pl.ds(r0, n), HZ + h0:HZ + h0 + HH, :]
+                            * (0.5 * cbuf[it, pl.ds(r0, n), HZ + h0:HZ + h0 + HH, :]))
+                    when(v == (1 - q if near else q), half)
+
+            for p in (1, 2, 3):
+                update(p)
+            leave(1, 0, NH)
+
+            def add_own():
+                sy_own(it, 0, False).wait_recv()
+                sy_own(it, 0, True).wait_recv()
+                cbuf[it, pl.ds(row(EDGE[0], my), my), HZ:HZ + NH, :] += rybuf[it, 0, :, HZ:HZ + NH, :]
+            with scope("Wown"):
+                when(has[0], add_own)
+            with scope("Wnear"):
+                finish(4, True)
+                finish(0, True)
+            leave(0, pl.multiple_of((1 - v) * HH, HH), HH)
+            with scope("Wfar"):
+                finish(4, False)
+                finish(0, False)
+            leave(0, pl.multiple_of(v * HH, HH), HH)
             with scope("Wsent2"):
                 sent()
             with scope("Wout"):
@@ -582,8 +642,8 @@
             vm((NR, NE, NX), F32), vm((2, 4, NY // 2 * NH, NX), BF16), vm((NY + 4 * my, NE, NX), F32),
             vm((ITERS, NR, NE, NX), F32), vm((ITERS, NR, NE, NX), F32),
             vm((ITERS, 2, my, NE, NX), F32), vm((ITERS, 2, NY, HZ, NX), F32), vm((ITERS, 2, my, HZ, NX), F32),
-            pltpu.SemaphoreType.DMA((5,)), pltpu.SemaphoreType.DMA((16,)), pltpu.SemaphoreType.DMA((32,)),
-            pltpu.SemaphoreType.DMA((2,)), pltpu.SemaphoreType.DMA((2,)),
+            pltpu.SemaphoreType.DMA((5,)), pltpu.SemaphoreType.DMA((18,)), pltpu.SemaphoreType.DMA((34,)),
+            pltpu.SemaphoreType.DMA((3,)), pltpu.SemaphoreType.DMA((3,)),
         ],
         compiler_params=pltpu.CompilerParams(
             collective_id=0, has_side_effects=True, vmem_limit_bytes=24 << 20),

time: 35.7 us -> 35.6 us (level)
  no operation moved by 1% of the time
where the time goes in v7:
time: 35.6 us; the launch traced here: 35.5 us
  Pallas kernels  35.4 us (99%)
    pallas_call x1, Pallas kernels, on_device(): pl.pallas_call(functools.partial(kernel, dims), out_shape=jax.ShapeDtypeS...  34.5 us
    pallas_call x1, Pallas kernels, on_device(): pl.pallas_call(store, out_shape=jax.ShapeDtypeStruct((NZ, NY, NX), F32),...  0.98 us

profile of v7, /device:TPU:13, one launch (start us, length us, event | category | flops | bytes accessed | tf_op | source)
XLA Modules:
  0.0 35.5 jit_solution(17985722142295110043)
XLA Ops:
  0.0 34.5 %shard_map.55.src = f32[64,16,256]{2,1,0:T(8,128)S(1)} custom-call(f32[1,64,16,256]{3,2,1,0:T(8,128)} %obs_hbm.1, f32[64,16,256]{2,1,0:T(8,128)} %start_hbm.1, f32[1,31]{1,0:T(1,128)} %sz_ref.1, f32[1,7]{1,0:T(1,128)} %sy_ref.1, f32[1,7]{1,0:T(1,128)} %sx_ref.1), custom_call_target="tpu_custom_call" | custom-call | tf_op jit(solution)/shard_map/pallas_call | solution.py:631
  34.5 1.0 %shard_map.56 = f32[64,16,256]{2,1,0:T(8,128)} custom-call(f32[64,16,256]{2,1,0:T(8,128)S(1)} %shard_map.55.src), custom_call_target="tpu_custom_call" | custom-call | tf_op jit(solution)/shard_map/pallas_call | solution.py:651

commit v8 on v7

--- a/solution.py
+++ b/solution.py
@@ -377,9 +377,7 @@
                 tx[view, back, 0, r0:r0 + 64, :] = high
                 tx[view, back, 1, r0:r0 + 64, :] = low
     wy = [[jnp.broadcast_to(tap(view, 1, b), (NH, NX)) for b in range(KY)] for view in range(2)]
-
-    qbuf[0:2 * my] = jnp.zeros((2 * my, NE, NX), F32)
-    qbuf[2 * my + NY:] = jnp.zeros((2 * my, NE, NX), F32)
+    wl = [[jnp.where(f == 0, wy[view][KY - 1 - k], wy[view][k]) for k in range(KY)] for view in range(2)]
 
     with scope("Wobs"):
         load_obs.wait()
@@ -430,15 +428,23 @@
 
         def crows(i0, n, it=it):
             with scope(f"c{it}_{i0}"):
+                inside = i0 >= 2 * my and i0 + n <= NY
                 r0 = row(i0, n)
                 for y in range(n):
-                    r = r0 + y
+                    r = r0 + y if inside else row(i0 + y)
                     parts = []
                     for view in range(2):
                         z0 = view * NH
-                        acc = wy[view][0] * qbuf[r + 2 * my, z0:z0 + NH, :]
-                        for b in range(1, KY):
-                            acc = acc + wy[view][b] * qbuf[r + 2 * my - b, z0:z0 + NH, :]
+                        acc = None
+                        for k in range(KY):
+                            o = i0 + y - 2 * my + k
+                            if inside:
+                                term = wy[view][k] * qbuf[r + 2 * my - k, z0:z0 + NH, :]
+                            elif 0 <= o < NY:
+                                term = wl[view][k] * qbuf[qrow(2 * my + o), z0:z0 + NH, :]
+                            else:
+                                continue
+                            acc = term if acc is None else acc + term
                         parts.append(acc)
                     cbuf[it, r] = jnp.dot(wb[...], stacked(jnp.concatenate(parts, axis=0)),
                                           preferred_element_type=F32)

time: 35.6 us -> 35.4 us (level)
  no operation moved by 1% of the time
where the time goes in v8:
time: 35.4 us; the launch traced here: 35.3 us
  Pallas kernels  35.3 us (100%)
    pallas_call x1, Pallas kernels, on_device(): pl.pallas_call(functools.partial(kernel, dims), out_shape=jax.ShapeDtypeS...  34.3 us
    pallas_call x1, Pallas kernels, on_device(): pl.pallas_call(store, out_shape=jax.ShapeDtypeStruct((NZ, NY, NX), F32),...  0.98 us

profile of v8, /device:TPU:13, one launch (start us, length us, event | category | flops | bytes accessed | tf_op | source)
XLA Modules:
  0.0 35.3 jit_solution(15591983625915217817)
XLA Ops:
  0.0 34.3 %shard_map.55.src = f32[64,16,256]{2,1,0:T(8,128)S(1)} custom-call(f32[1,64,16,256]{3,2,1,0:T(8,128)} %obs_hbm.1, f32[64,16,256]{2,1,0:T(8,128)} %start_hbm.1, f32[1,31]{1,0:T(1,128)} %sz_ref.1, f32[1,7]{1,0:T(1,128)} %sy_ref.1, f32[1,7]{1,0:T(1,128)} %sx_ref.1), custom_call_target="tpu_custom_call" | custom-call | tf_op jit(solution)/shard_map/pallas_call | solution.py:637
  34.3 1.0 %shard_map.56 = f32[64,16,256]{2,1,0:T(8,128)} custom-call(f32[64,16,256]{2,1,0:T(8,128)S(1)} %shard_map.55.src), custom_call_target="tpu_custom_call" | custom-call | tf_op jit(solution)/shard_map/pallas_call | solution.py:657

commit v9 on v8

--- a/solution.py
+++ b/solution.py
@@ -118,9 +118,10 @@
             src_ref=src, dst_ref=dst, send_sem=ssem.at[send], recv_sem=rsem.at[recv],
             device_id=to, device_id_type=MESH)
 
-    ROWS = ((NY, my), (my, my + 1), (2 * my + 1, NY - 4 * my - 1), (NY - 2 * my, my), (NY - my, my))
+    ROWS = ((NY, my), (my, my + 1), (2 * my + 1, NY - 4 * my - 1), (NY - 2 * my, my), (NY - my, my), (NY - my, 2 * my))
+    LAST = NP
     OUT, MID = NY - 3 * my, 2 * my
-    assert len(ROWS) == NP
+    assert len(ROWS) == NP + 1
     ZED = ((HZ, NH), (0, HZ), (HZ + NH, HZ))
     zed_has = (None, dn_z, up_z)
     EDGE, HALO = (NY, my), (my + NY, 0)
@@ -169,7 +170,8 @@
         src0 = (HZ + NH, 0)[d]
         n = ROWS[p][1]
         r0 = row(*ROWS[p])
-        return copy(NP * d + p, 2 * NP + NP * d + p, cbuf.at[it, pl.ds(r0, n), pl.ds(src0, HZ)],
+        k = NP * d + p % NP
+        return copy(k, 2 * NP + k, cbuf.at[it, pl.ds(r0, n), pl.ds(src0, HZ)],
                     rzbuf.at[it, d, pl.ds(r0 - my, n)], zto[d])
 
     def sy(it, d, p):
@@ -187,7 +189,7 @@
         follow(sz(it - 1, d, p), gz(it, d, p))
 
     def send_sz(it, d, p):
-        follow(gz(it, d, p) if it > 0 else first(d, p) if p < 2 else None, sz(it, d, p))
+        follow(gz(it, d, p % NP) if it > 0 else first(d, p) if p < 2 else None, sz(it, d, p))
 
     def send_gy(it, d, p):
         before = None if it == 0 else sy_own(it - 1, d, False) if p == 0 else sy(it - 1, d, p)
@@ -253,7 +255,8 @@
         it = ITERS - 1
         for d in range(2):
             def along_z(d=d):
-                for p in range(NP):
+                gz(it, d, 4).wait_send()
+                for p in (1, 2, 3, LAST):
                     sz(it, d, p).wait_send()
             when(zhas[d], along_z)
 
@@ -523,8 +526,7 @@
             qrows(OUT + MID, my)
             when(has[0], high_scatter)
             crows(NY - my, 2 * my)
-            scatter_piece(it, 0)
-            scatter_piece(it, 4)
+            scatter_piece(it, LAST)
             with scope(f"Wso{it}"):
                 scatter_own(it, 0)
 
@@ -583,11 +585,11 @@
                             sz(it, q, p).wait_recv()
                             cbuf[it, pl.ds(r0, n), z0:z0 + HZ, :] += rzbuf[it, q, pl.ds(r0 - my, n)]
                         when(zfrom[q], add)
-                        if p == 0 and not near:
+                        if not near:
                             def add_diagonal():
-                                diagonal(it, p, 1 - q).wait_recv()
-                                cbuf[it, pl.ds(row(EDGE[p], my), my), z0:z0 + HZ, :] += rybuf[it, p, :, 0:HZ, :]
-                            when(both(zfrom[q], has[p]), add_diagonal)
+                                diagonal(it, 0, 1 - q).wait_recv()
+                                cbuf[it, pl.ds(row(EDGE[0], my), my), z0:z0 + HZ, :] += rybuf[it, 0, :, 0:HZ, :]
+                            when(both(zfrom[q], has[0]), add_diagonal)
                         zbuf[pl.ds(r0, n), h0:h0 + HH, :] = (
                             ebuf[it, pl.ds(r0, n), HZ + h0:HZ + h0 + HH, :]
                             * (0.5 * cbuf[it, pl.ds(r0, n), HZ + h0:HZ + h0 + HH, :]))
@@ -604,12 +606,10 @@
             with scope("Wown"):
                 when(has[0], add_own)
             with scope("Wnear"):
-                finish(4, True)
-                finish(0, True)
+                finish(LAST, True)
             leave(0, pl.multiple_of((1 - v) * HH, HH), HH)
             with scope("Wfar"):
-                finish(4, False)
-                finish(0, False)
+                finish(LAST, False)
             leave(0, pl.multiple_of(v * HH, HH), HH)
             with scope("Wsent2"):
                 sent()

time: 35.4 us -> 35.4 us (level)
  no operation moved by 1% of the time
where the time goes in v9:
time: 35.4 us; the launch traced here: 35.2 us
  Pallas kernels  35.2 us (99%)
    pallas_call x1, Pallas kernels, on_device(): pl.pallas_call(functools.partial(kernel, dims), out_shape=jax.ShapeDtypeS...  34.3 us
    pallas_call x1, Pallas kernels, on_device(): pl.pallas_call(store, out_shape=jax.ShapeDtypeStruct((NZ, NY, NX), F32),...  0.98 us

profile of v9, /device:TPU:13, one launch (start us, length us, event | category | flops | bytes accessed | tf_op | source)
XLA Modules:
  0.0 35.2 jit_solution(16178696554377812059)
XLA Ops:
  0.0 34.3 %shard_map.55.src = f32[64,16,256]{2,1,0:T(8,128)S(1)} custom-call(f32[1,64,16,256]{3,2,1,0:T(8,128)} %obs_hbm.1, f32[64,16,256]{2,1,0:T(8,128)} %start_hbm.1, f32[1,31]{1,0:T(1,128)} %sz_ref.1, f32[1,7]{1,0:T(1,128)} %sy_ref.1, f32[1,7]{1,0:T(1,128)} %sx_ref.1), custom_call_target="tpu_custom_call" | custom-call | tf_op jit(solution)/shard_map/pallas_call | solution.py:637
  34.3 1.0 %shard_map.56 = f32[64,16,256]{2,1,0:T(8,128)} custom-call(f32[64,16,256]{2,1,0:T(8,128)S(1)} %shard_map.55.src), custom_call_target="tpu_custom_call" | custom-call | tf_op jit(solution)/shard_map/pallas_call | solution.py:657

commit v10 on v8

--- a/solution.py
+++ b/solution.py
@@ -500,8 +500,9 @@
             when(has[0], high_edge)
             qrows(OUT + MID, my)
             when(has[0], high_scatter)
-            crows(NY - my, 2 * my)
+            crows(*ROWS[4])
             scatter_piece(it, 4)
+            crows(*ROWS[0])
             scatter_near(it, 0)
             with scope(f"Wso{it}"):
                 scatter_own(it, 0)

time: 35.4 us -> 35.4 us (level)
  no operation moved by 1% of the time
where the time goes in v10:
time: 35.4 us; the launch traced here: 35.3 us
  Pallas kernels  35.3 us (100%)
    pallas_call x1, Pallas kernels, on_device(): pl.pallas_call(functools.partial(kernel, dims), out_shape=jax.ShapeDtypeS...  34.3 us
    pallas_call x1, Pallas kernels, on_device(): pl.pallas_call(store, out_shape=jax.ShapeDtypeStruct((NZ, NY, NX), F32),...  0.98 us

profile of v10, /device:TPU:13, one launch (start us, length us, event | category | flops | bytes accessed | tf_op | source)
XLA Modules:
  0.0 35.3 jit_solution(6259696114574722941)
XLA Ops:
  0.0 34.3 %shard_map.55.src = f32[64,16,256]{2,1,0:T(8,128)S(1)} custom-call(f32[1,64,16,256]{3,2,1,0:T(8,128)} %obs_hbm.1, f32[64,16,256]{2,1,0:T(8,128)} %start_hbm.1, f32[1,31]{1,0:T(1,128)} %sz_ref.1, f32[1,7]{1,0:T(1,128)} %sy_ref.1, f32[1,7]{1,0:T(1,128)} %sx_ref.1), custom_call_target="tpu_custom_call" | custom-call | tf_op jit(solution)/shard_map/pallas_call | solution.py:638
  34.3 1.0 %shard_map.56 = f32[64,16,256]{2,1,0:T(8,128)} custom-call(f32[64,16,256]{2,1,0:T(8,128)S(1)} %shard_map.55.src), custom_call_target="tpu_custom_call" | custom-call | tf_op jit(solution)/shard_map/pallas_call | solution.py:658
